TPU v7x, 128 devices: a whole 4x4x4 slice. The times are simulated.
128 devices in a mesh: patch: 16 (over y, x_lo, core), tensor: 8 (over z, x_hi).
Axes of the slice: x: 4 (x_hi: 2, x_lo: 2; x = x_hi * 2 + x_lo), y: 4, z: 4, core: 2. Of those that a mesh axis runs over, the one named last changes fastest.
Arguments:
- patches: float32 [4096, 768], P('patch'), may hold values from -6 to 6
- perms: int32 [2, 768], replicated, may hold values from 0 to 767, each once within a row
- w_in: float32 [2, 384, 1024], replicated, may hold values from -0.3125 to 0.3125
- gain_mix: float32 [2, 1024], replicated, may hold values from 0.5 to 1.5
- w_qkv: float32 [2, 1024, 3, 1024], P(None, None, None, 'tensor'), may hold values from -8 to 8
- w_mix: float32 [2, 1024, 1024], P(None, 'tensor'), may hold values from -0.1875 to 0.1875
- gain_out: float32 [2, 1024], replicated, may hold values from 0.5 to 1.5
- w_head: float32 [2, 1024, 768], P(None, 'tensor'), may hold values from -0.1875 to 0.1875
- order: int32 [4096], P('patch'), may hold values from 0 to 4095, as said below
- w_embed: bfloat16 [768, 2048], P(None, 'tensor'), may hold values from -0.21875 to 0.21875
- gain_attn: float32 [2048], replicated, may hold values from 0.5 to 1.5
- w_query: bfloat16 [2048, 2048], P(None, 'tensor'), may hold values from -5.656854 to 5.656854
- w_keyval: bfloat16 [2048, 512], replicated, may hold values from -0.125 to 0.125
- w_attn: bfloat16 [2048, 2048], P('tensor'), may hold values from -0.125 to 0.125
- gain_mlp: float32 [2048], replicated, may hold values from 0.5 to 1.5
- w_gate: bfloat16 [2048, 8192], P(None, 'tensor'), may hold values from -0.125 to 0.125
- w_up: bfloat16 [2048, 8192], P(None, 'tensor'), may hold values from -0.125 to 0.125
- w_down: bfloat16 [8192, 2048], P('tensor'), may hold values from -0.0625 to 0.0625
Outputs:
- decoded: bfloat16 [4096, 2048], P('patch', 'tensor')
- logdet: float32 [4096], P('patch')
Inputs may be any that keep to these rules, and one draw needn't show every extreme that they name: `order`: a permutation of all positions; the tokens of each aligned block of 64 hold exactly that block's positions. `perms`: each row holds every channel once.
All inputs are finite; a program needn't handle non-finite values.
Results may differ from a plain program's by a relative error of at most 0.015.
The roundings to bfloat16 on the way count: a program that leaves them out, or rounds other values in their place, can miss the bound.
Values may be sent and summed in bfloat16 or wider, within the bound.
No kernel may reach another device: no remote copies, remote signals or barrier semaphores. Data moves between devices by JAX's collectives and lax.ppermute only.
A program may use at most 128 MiB of HBM per device.

v0:
```python
import functools

import jax
import jax.numpy as jnp
from jax import lax
from jax.experimental import pallas as pl
from jax.experimental.pallas import tpu as pltpu
from jax.sharding import PartitionSpec as P


BLOCKS = 2
DH = 256
NP = 16
NT = 8


highest = lax.Precision.HIGHEST
bf16 = jnp.bfloat16
f32 = jnp.float32


def normed(value, gain):
    return value * lax.rsqrt(jnp.mean(value * value, axis=-1, keepdims=True) + 1e-06) * gain


def mm32(left, right):
    return jnp.dot(left, right, precision=highest, preferred_element_type=f32)


CORE = [(i, i ^ 1) for i in range(NP)]


def hop(dy, dx):
    def to(i):
        y, x, c = i // 4, (i // 2) % 2, i % 2
        return ((y + dy) % 4 * 2 + (x + dx) % 2) * 2 + c

    return [(i, to(i)) for i in range(NP)]


UP, DOWN, SIDE = hop(1, 0), hop(-1, 0), hop(0, 1)


def over(value, pairs):
    return lax.ppermute(value, "patch", pairs)


def gather_chips(own):
    half = own.shape[0] // 2
    up = over(own, UP)
    down = over(own, DOWN)
    side = over(own, SIDE)
    side_up = over(side, UP)
    side_down = over(down, SIDE)
    far_a = over(up[:half], UP)
    far_b = over(down[half:], DOWN)
    far = jnp.concatenate([far_a, far_b], 0)
    side_far = over(far, SIDE)
    return [own, up, down, side, side_up, side_down, far, side_far]


def exchange(parts):
    return lax.all_to_all(parts, "tensor", 0, 0)


def split2(x):
    a = x.astype(bf16)
    b = (x - a.astype(f32)).astype(bf16)
    return a, b


def split3(x):
    a = x.astype(bf16)
    r = x - a.astype(f32)
    b = r.astype(bf16)
    c = (r - b.astype(f32)).astype(bf16)
    return a, b, c


def select(x, one_hot):
    return sum(jnp.dot(p, one_hot, preferred_element_type=f32) for p in reversed(split3(x)))


VMEM = pl.BlockSpec(memory_space=pltpu.VMEM)
SMEM = pl.BlockSpec(memory_space=pltpu.SMEM)


def call(body, outs, *args, scratch=(), flops=0, limit=40, smem=0):
    moved = sum(x.size * x.dtype.itemsize for x in args)
    return pl.pallas_call(
        body,
        in_specs=[SMEM] * smem + [VMEM] * (len(args) - smem),
        out_specs=[VMEM] * len(outs),
        out_shape=[jax.ShapeDtypeStruct(*o) for o in outs],
        scratch_shapes=list(scratch),
        compiler_params=pltpu.CompilerParams(vmem_limit_bytes=limit << 20),
        cost_estimate=pl.CostEstimate(flops=flops, bytes_accessed=moved, transcendentals=0),
    )(*args)


def pre_kernel(ids, field_ref, perm_ref, w_in_ref, gain_ref, w_ref, hidden_ref, q_ref, kv_ref, oth_ref):
    even = ids[0] == 0
    half = w_in_ref.shape[0]
    width = field_ref.shape[1]
    lanes = w_ref.shape[1] // 3
    hd = lanes // 2
    row = lax.broadcasted_iota(jnp.int32, (width, half), 0)
    take = jnp.where(row == perm_ref[...], 1.0, 0.0).astype(bf16)
    cond = select(field_ref[...], take)
    hidden = mm32(cond, w_in_ref[...])
    hidden_ref[...] = hidden
    unit = normed(hidden, gain_ref[...])
    qkv = mm32(unit, w_ref[...])

    def pick(i, first):
        x = qkv[:, i * lanes : (i + 1) * lanes]
        return jnp.where(first, x[:, :hd], x[:, hd:])

    q_ref[...] = pick(0, even)
    kv_ref[...] = jnp.concatenate([pick(1, even), pick(2, even)], axis=1)
    odd = jnp.logical_not(even)
    oth_ref[...] = jnp.concatenate([pick(0, odd), pick(1, odd), pick(2, odd)], axis=1)


def pre(ids, field, perm, w_in, gain, w_qkv):
    rows, full = field.shape[0], w_in.shape[1]
    lanes = w_qkv.shape[1] // 3
    hd = lanes // 2
    return call(
        pre_kernel,
        [((rows, full), f32), ((rows, hd), f32), ((rows, 2 * hd), f32), ((rows, 3 * hd), f32)],
        ids,
        field,
        perm[None, : w_in.shape[0]],
        w_in,
        gain[None],
        w_qkv,
        smem=1,
        flops=3 << 30,
    )


def attend_kernel(count, first, last, q_ref, *refs):
    kv_refs, refs = refs[:count], refs[count:]
    if not first:
        (acc0_ref, top0_ref, sum0_ref), refs = refs[:3], refs[3:]
    hd = q_ref.shape[1]
    s_ref = refs[-1]
    q1, q2, q3 = split3(q_ref[...] * (hd ** (-0.5)))
    qs = jnp.concatenate([q1, q1, q2, q1, q2, q3], axis=1)
    top = None if first else top0_ref[...]
    for j, kv_ref in enumerate(kv_refs):
        k1, k2, k3 = split3(kv_ref[:, :hd])
        ks = jnp.concatenate([k1, k2, k1, k3, k2, k1], axis=1)
        s = lax.dot_general(qs, ks, (((1,), (1,)), ((), ())), preferred_element_type=f32)
        s_ref[j] = s
        m = jnp.max(s, axis=1, keepdims=True)
        top = m if top is None else jnp.maximum(top, m)
    total = acc = None
    if not first:
        factor = jnp.exp(top0_ref[...] - top)
        total, acc = sum0_ref[...] * factor, acc0_ref[...] * factor
    for j, kv_ref in enumerate(kv_refs):
        p = jnp.exp(s_ref[j] - top)
        t = jnp.sum(p, axis=1, keepdims=True)
        v1, v2, v3 = split3(kv_ref[:, hd:])
        p1, p2 = split2(p)
        a = jnp.dot(p1, jnp.concatenate([v1, v2, v3], axis=1), preferred_element_type=f32)
        b = jnp.dot(p2, jnp.concatenate([v1, v2], axis=1), preferred_element_type=f32)
        a = a[:, :hd] + (a[:, hd : 2 * hd] + b[:, :hd]) + (a[:, 2 * hd :] + b[:, hd:])
        total = t if total is None else total + t
        acc = a if acc is None else acc + a
    if last:
        refs[0][...] = acc / total
    else:
        refs[0][...] = acc
        refs[1][...] = top
        refs[2][...] = total


def attend(query, pieces, state, last):
    rows, hd = query.shape
    keys = pieces[0].shape[0]
    block = 256
    count = len(pieces)

    def by_rows(cols):
        return pl.BlockSpec((block, cols), lambda i: (i, 0))

    widths = (hd,) if last else (hd, 1, 1)
    state_specs = [by_rows(hd), by_rows(1), by_rows(1)] if state else []
    return pl.pallas_call(
        functools.partial(attend_kernel, count, not state, last),
        grid=(rows // block,),
        in_specs=[by_rows(hd)]
        + [pl.BlockSpec((keys, 2 * hd), lambda i: (0, 0))] * count
        + state_specs,
        out_specs=[by_rows(w) for w in widths],
        out_shape=[jax.ShapeDtypeStruct((rows, w), f32) for w in widths],
        scratch_shapes=[pltpu.VMEM((count, block, keys), f32)],
        compiler_params=pltpu.CompilerParams(vmem_limit_bytes=32 << 20),
        cost_estimate=pl.CostEstimate(
            flops=4 << 30, bytes_accessed=count * keys * hd * 8, transcendentals=rows * keys * count
        ),
        name="attend",
    )(query, *pieces, *state)


def post_kernel(ids, m_ref, own_ref, oth_ref, hidden_ref, field_ref, perm_ref, gain_ref, out_ref, det_ref):
    even = ids[0] == 0
    nt, _, lanes = m_ref.shape
    full, width = hidden_ref.shape[1], field_ref.shape[1]
    half, mid = width // 2, full // 2
    mixed = jnp.concatenate([m_ref[t] for t in range(nt)], axis=1)

    def product(left, lo, hi):
        a = mm32(left, own_ref[:, :, lo:hi].reshape(nt * lanes, hi - lo))
        b = mm32(left, oth_ref[:, :, lo:hi].reshape(nt * lanes, hi - lo))
        return jnp.where(even, a, b), jnp.where(even, b, a)

    hidden = hidden_ref[...] + jnp.concatenate(product(mixed, 0, mid), axis=1)
    raw, shift = product(normed(hidden, gain_ref[...]), mid, mid + half)
    log_scale = jnp.tanh(raw)
    det_ref[...] = jnp.sum(log_scale, axis=1, keepdims=True)
    col = lax.broadcasted_iota(jnp.int32, (half, width), 1)
    put = jnp.where(col == perm_ref[...], 1.0, 0.0).astype(bf16)
    field = field_ref[...] * jnp.exp(select(log_scale, put)) + select(shift, put)
    out_ref[...] = field.astype(out_ref.dtype)


def post(ids, mixed, own, oth, hidden, field, perm, gain, kind):
    rows, width = field.shape
    return call(
        post_kernel,
        [((rows, width), kind), ((rows, 1), f32)],
        ids,
        mixed,
        own,
        oth,
        hidden,
        field,
        perm[width // 2 :, None],
        gain[None],
        smem=1,
        flops=6 << 30,
    )


def enter_kernel(emb_ref, gain_ref, w_query_ref, w_keyval_ref, q_ref, kv_ref):
    start = jnp.concatenate([emb_ref[t] for t in range(emb_ref.shape[0])], axis=1)
    unit = normed(start.astype(f32), gain_ref[...]).astype(bf16)
    kv_ref[...] = jnp.dot(unit, w_keyval_ref[...], preferred_element_type=f32).astype(bf16)
    q_ref[...] = jnp.dot(unit, w_query_ref[...], preferred_element_type=f32).astype(bf16)


def causal_kernel(ids, q_ref, order_ref, order_row_ref, *refs):
    kv_refs, o_ref, s_ref = refs[:-2], refs[-2], refs[-1]
    dh = q_ref.shape[1]
    patch = ids[1]
    own = order_row_ref[...] <= order_ref[...]
    top = None
    for j, kv_ref in enumerate(kv_refs):
        owner = ids[2 + j]
        s = lax.dot_general(
            q_ref[...], kv_ref[:, :dh], (((1,), (1,)), ((), ())), preferred_element_type=f32
        ) * (dh ** (-0.5))
        if j == 0:
            s = jnp.where(own, s, -jnp.inf)
        else:
            s = jnp.where(owner < patch, s, -jnp.inf)
        s_ref[j] = s
        m = jnp.max(s, axis=1, keepdims=True)
        top = m if top is None else jnp.maximum(top, m)
    total = acc = None
    for j, kv_ref in enumerate(kv_refs):
        p = jnp.exp(s_ref[j] - top)
        t = jnp.sum(p, axis=1, keepdims=True)
        a = jnp.dot(p.astype(bf16), kv_ref[:, dh:], preferred_element_type=f32)
        total = t if total is None else total + t
        acc = a if acc is None else acc + a
    o_ref[...] = (acc / total).astype(bf16)


def mlp_kernel(
    ids, att_ref, emb_ref, own_ref, oth_ref, gain_ref, gate_ref, up_ref, down_ref,
    out_ref, resid_ref, full_ref, inner_ref,
):
    even = ids[0] == 0
    nt, _, lanes = att_ref.shape
    half = own_ref.shape[2]
    att = jnp.concatenate([att_ref[t] for t in range(nt)], axis=1)
    tile = 256

    for start in range(0, half, tile):
        a = jnp.dot(att, own_ref[:, :, start : start + tile].reshape(-1, tile), preferred_element_type=f32)
        b = jnp.dot(att, oth_ref[:, :, start : start + tile].reshape(-1, tile), preferred_element_type=f32)
        for x, at in ((jnp.where(even, a, b), start), (jnp.where(even, b, a), half + start)):
            full_ref[:, at : at + tile] = x + emb_ref[at // lanes].astype(f32)
    mine = pl.multiple_of(ids[1] * lanes, lanes)
    resid_ref[...] = full_ref[:, pl.ds(mine, lanes)]
    unit = normed(full_ref[...], gain_ref[...]).astype(bf16)
    for start in range(0, gate_ref.shape[1], tile):
        cut = slice(start, start + tile)
        gate = jnp.dot(unit, gate_ref[:, cut], preferred_element_type=f32)
        up = jnp.dot(unit, up_ref[:, cut], preferred_element_type=f32)
        inner_ref[:, cut] = (jax.nn.gelu(gate, approximate=True) * up).astype(bf16)
    for t in range(nt):
        out_ref[t] = jnp.dot(
            inner_ref[...], down_ref[:, t * lanes : (t + 1) * lanes], preferred_element_type=f32
        ).astype(bf16)


def tied(value, *others):
    return lax.optimization_barrier((value, *others))[0]


def on_device(
    patches,
    perms,
    w_in,
    gain_mix,
    w_qkv,
    w_mix,
    gain_out,
    w_head,
    order,
    w_embed,
    gain_attn,
    w_query,
    w_keyval,
    w_attn,
    gain_mlp,
    w_gate,
    w_up,
    w_down,
):
    rows = patches.shape[0]
    full = w_in.shape[2]
    local_w = w_qkv.shape[3]
    where = lax.axis_index("tensor")
    patch = lax.axis_index("patch")
    core = patch % 2
    even = core == 0
    ids = jnp.stack([core, where]).astype(jnp.int32)

    def halves(x):
        cols = x.shape[1] // 2
        return lax.dynamic_slice_in_dim(x, core * cols, cols, 1)

    field = patches
    logdet = 0.0
    for blk in range(BLOCKS):
        perm = perms[blk]
        hidden, query, keyval, other = pre(
            ids, field, perm, w_in[blk], gain_mix[blk], w_qkv[blk].reshape(full, 3 * local_w)
        )
        hd = local_w // 2
        got = over(other, CORE)
        query = jnp.concatenate([query, got[:, :hd]], axis=0)
        keyval = jnp.concatenate([keyval, got[:, hd:]], axis=0)
        weight = jnp.concatenate([halves(w_mix[blk]), halves(w_head[blk])], axis=1)
        weight = tied(weight, keyval)
        own_w = exchange(jnp.broadcast_to(weight, (NT,) + weight.shape))
        oth_w = over(own_w, CORE)
        pieces = gather_chips(keyval)
        state = attend(query, pieces[:4], [], False)
        (out,) = attend(query, pieces[4:], state, True)
        back = over(out[rows:], CORE)
        front = out[:rows]
        mixed = jnp.concatenate(
            [jnp.where(even, front, back), jnp.where(even, back, front)], axis=1
        )
        mixed = tied(mixed, own_w)
        mixed = exchange(jnp.broadcast_to(mixed, (NT,) + mixed.shape))
        field, det = post(
            ids, mixed, own_w, oth_w, hidden, field, perm, gain_out[blk],
            bf16 if blk == BLOCKS - 1 else f32,
        )
        logdet = logdet + det[:, 0]
    embed_part = jnp.dot(field, w_embed, preferred_element_type=f32).astype(bf16)
    embedded = exchange(jnp.broadcast_to(embed_part, (NT,) + embed_part.shape))
    query_dec, keyval = call(
        enter_kernel,
        [((rows, DH), bf16), ((rows, 2 * DH), bf16)],
        embedded,
        gain_attn[None],
        w_query,
        w_keyval,
        flops=1 << 30,
    )
    attn_half = tied(halves(w_attn), keyval)
    own_a = exchange(jnp.broadcast_to(attn_half, (NT,) + attn_half.shape))
    oth_a = over(own_a, CORE)
    pieces = gather_chips(keyval)
    pieces = pieces + [over(x, CORE) for x in pieces]

    y, x = patch // 4, (patch // 2) % 2
    owners = [core, patch]
    for dc in (0, 1):
        for dy, dx in ((0, 0), (-1, 0), (1, 0), (0, 1), (-1, 1), (1, 1), (2, 0), (2, 1)):
            owners.append((((y + dy) % 4) * 2 + (x + dx) % 2) * 2 + (core + dc) % 2)
    (attended,) = call(
        causal_kernel,
        [((rows, DH), bf16)],
        jnp.stack(owners).astype(jnp.int32),
        query_dec,
        order[:, None],
        order[None],
        *pieces,
        scratch=[pltpu.VMEM((len(pieces), rows, rows), f32)],
        smem=1,
        flops=2 << 30,
    )
    attended = tied(attended, own_a)
    att = exchange(jnp.broadcast_to(attended, (NT,) + attended.shape))
    cols = w_attn.shape[1] // NT
    down, resid = call(
        mlp_kernel,
        [((NT, rows, cols), bf16), ((rows, cols), f32)],
        ids,
        att,
        embedded,
        own_a,
        oth_a,
        gain_mlp[None],
        w_gate,
        w_up,
        w_down,
        scratch=[
            pltpu.VMEM((rows, w_attn.shape[1]), f32),
            pltpu.VMEM((rows, w_gate.shape[1]), bf16),
        ],
        smem=1,
        flops=6 << 30,
    )
    decoded = (jnp.sum(exchange(down).astype(f32), axis=0) + resid).astype(bf16)
    return (decoded, logdet)


def solution(mesh):
    return jax.shard_map(
        on_device,
        mesh=mesh,
        in_specs=(
            P("patch", None),
            P(),
            P(),
            P(),
            P(None, None, None, "tensor"),
            P(None, "tensor", None),
            P(),
            P(None, "tensor", None),
            P("patch"),
            P(None, "tensor"),
            P(),
            P(None, "tensor"),
            P(),
            P("tensor", None),
            P(),
            P(None, "tensor"),
            P(None, "tensor"),
            P("tensor", None),
        ),
        out_specs=(P("patch", "tensor"), P("patch")),
        check_vma=False,
    )
```

profile of v0, /device:TPU:0, one launch (start us, length us, event | category | flops | bytes accessed | tf_op | source)
XLA Modules:
  0.0 465.4 jit_solution(14069800608825800845)
XLA Ops:
  1.5 4.1 slice_bitcast_fusion
  13.1 5.1 %shard_map.185 = (f32[256,1024]{1,0:T(8,128)S(1)}, f32[256,64]{1,0:T(8,128)S(1)}, f32[256,128]{1,0:T(8,128)S(1)}, f32[256,192]{1,0:T(8,128)S(1)}) custom-call(s32[2]{0:T(128)S(1)} %pad_add_fusion.ids, f32[256,768]{1,0:T(8,128)S(1)} %copy-done.7, s32[1,384]{1,0:T(1,128)S(1)} %get-tuple-element.76.perm_ref, f32[384,1024]{1,0:T(8,128)S(1)} %copy-done.3, ...), custom_call_target="tpu_custom_call" | custom-call | flops 3221225472 | bytes 3937800 | tf_op jit(solution)/shard_map/pallas_call | solution.py:90
  22.6 53.8 %all_to_all.40.own_ref = f32[8,128,896]{2,1,0:T(8,128)} all-to-all(f32[8,128,896]{2,1,0:T(8,128)S(1)} %broadcast_in_dim.41), channel_id=1, replica_groups=mesh['patch'=16,'tensor'=8] {'tensor'}, dimensions={0} | all-to-all | bytes 7340032 | tf_op jit(solution)/shard_map/all_to_all | solution.py:63
  80.2 6.2 %collective-permute-done.5.refs_1_ = f32[512,128]{1,0:T(8,128)S(1)} collective-permute-done((f32[512,128]{1,0:T(8,128)S(1)}, f32[512,128]{1,0:T(8,128)S(1)}, u32[]{:S(2)}, u32[]{:S(2)}) %collective-permute-start.5) | collective-permute-done | bytes 262176 | tf_op jit(solution)/shard_map/ppermute | solution.py:45
  93.7 4.2 attend.4
  99.1 3.8 collective-permute-done.8.refs_3_
  102.9 7.0 %attend.5 = f32[512,64]{1,0:T(8,128)S(1)} custom-call(f32[512,64]{1,0:T(8,128)S(1)} %pad_maximum_fusion.2.q_ref, f32[512,128]{1,0:T(8,128)S(1)} %collective-permute-done.2.refs_0_, f32[512,128]{1,0:T(8,128)S(1)} %collective-permute-done.4.refs_1_, f32[512,128]{1,0:T(8,128)S(1)} %constant_dynamic-update-slice_fusion.refs_2_, ...), custom_call_target="tpu_custom_call" | custom-call | flops 4294967296 | bytes 1048576 | tf_op jit(solution)/shard_map/attend/pallas_call | solution.py:192
  112.5 4.2 all-to-all-start.1
  122.7 11.9 %all-to-all-done.1.m_ref = f32[8,256,128]{2,1,0:T(8,128)} async-done(((f32[8,256,128]{2,1,0:T(8,128)}), f32[8,256,128]{2,1,0:T(8,128)}, u32[]{:S(2)}, u32[]{:S(2)}) %all-to-all-start.1) | async-done | bytes 1048608 | tf_op jit(solution)/shard_map/all_to_all | solution.py:63
  136.9 13.0 %shard_map.186 = (f32[256,768]{1,0:T(8,128)S(1)}, f32[256,1]{1,0:T(8,128)S(1)}) custom-call(s32[2]{0:T(128)S(1)} %pad_add_fusion.ids, f32[8,256,128]{2,1,0:T(8,128)} %all-to-all-done.1.m_ref, f32[8,128,896]{2,1,0:T(8,128)} %all_to_all.40.own_ref, f32[8,128,896]{2,1,0:T(8,128)} %collective-permute-done.10.oth_ref, f32[256,1024]{1,0:T(8,128)S(1)} %copy-done.23, ...), custom_call_target="tpu_custom_call" | custom-call | flops 6442450944 | bytes 10229256 | tf_op jit(solution)/shard_map/pallas_call | solution.py:90
  150.0 13.0 %shard_map.187 = (f32[256,1024]{1,0:T(8,128)S(1)}, f32[256,64]{1,0:T(8,128)S(1)}, f32[256,128]{1,0:T(8,128)S(1)}, f32[256,192]{1,0:T(8,128)S(1)}) custom-call(s32[2]{0:T(128)S(1)} %pad_add_fusion.ids, f32[256,768]{1,0:T(8,128)S(1)} %get-tuple-element.39.field_ref, s32[1,384]{1,0:T(1,128)S(1)} %get-tuple-element.77.perm_ref, f32[384,1024]{1,0:T(8,128)S(1)} %copy-done.2, ...), custom_call_target="tpu_custom_call" | custom-call | flops 3221225472 | bytes 3937800 | tf_op jit(solution)/shard_map/pallas_call | solution.py:90
  165.0 49.1 %all_to_all.41.own_ref = f32[8,128,896]{2,1,0:T(8,128)} all-to-all(f32[8,128,896]{2,1,0:T(8,128)S(1)} %broadcast_in_dim.44), channel_id=1, replica_groups=mesh['patch'=16,'tensor'=8] {'tensor'}, dimensions={0} | all-to-all | bytes 7340032 | tf_op jit(solution)/shard_map/all_to_all | solution.py:63
  218.0 6.1 %collective-permute-done.16.refs_1_ = f32[512,128]{1,0:T(8,128)S(1)} collective-permute-done((f32[512,128]{1,0:T(8,128)S(1)}, f32[512,128]{1,0:T(8,128)S(1)}, u32[]{:S(2)}, u32[]{:S(2)}) %collective-permute-start.16) | collective-permute-done | bytes 262176 | tf_op jit(solution)/shard_map/ppermute | solution.py:45
  224.2 3.3 collective-permute-start.18
  231.1 4.2 attend.6
  236.8 3.7 collective-permute-done.19.refs_3_
  240.5 7.0 %attend.7 = f32[512,64]{1,0:T(8,128)S(1)} custom-call(f32[512,64]{1,0:T(8,128)S(1)} %pad_maximum_fusion.4.q_ref, f32[512,128]{1,0:T(8,128)S(1)} %collective-permute-done.13.refs_0_, f32[512,128]{1,0:T(8,128)S(1)} %collective-permute-done.15.refs_1_, f32[512,128]{1,0:T(8,128)S(1)} %constant_dynamic-update-slice_fusion.2.refs_2_, ...), custom_call_target="tpu_custom_call" | custom-call | flops 4294967296 | bytes 1048576 | tf_op jit(solution)/shard_map/attend/pallas_call | solution.py:192
  250.2 3.8 all-to-all-start.3
  254.1 17.6 %all-to-all-done.3.m_ref = f32[8,256,128]{2,1,0:T(8,128)S(1)} async-done(((f32[8,256,128]{2,1,0:T(8,128)}), f32[8,256,128]{2,1,0:T(8,128)S(1)}, u32[]{:S(2)}, u32[]{:S(2)}) %all-to-all-start.3) | async-done | bytes 1048608 | tf_op jit(solution)/shard_map/all_to_all | solution.py:63
  274.1 12.6 %shard_map.188 = (bf16[256,768]{1,0:T(8,128)(2,1)S(1)}, f32[256,1]{1,0:T(8,128)S(1)}) custom-call(s32[2]{0:T(128)S(1)} %pad_add_fusion.ids, f32[8,256,128]{2,1,0:T(8,128)S(1)} %all-to-all-done.3.m_ref, f32[8,128,896]{2,1,0:T(8,128)} %all_to_all.41.own_ref, f32[8,128,896]{2,1,0:T(8,128)} %collective-permute-done.21.oth_ref, f32[256,1024]{1,0:T(8,128)S(1)} %copy-done.25, ...), custom_call_target="tpu_custom_call" | custom-call | flops 6442450944 | bytes 10229256 | tf_op jit(solution)/shard_map/pallas_call | solution.py:90
  288.0 3.6 all-to-all-start.4
  292.4 15.9 %all-to-all-done.4.emb_ref = bf16[8,256,256]{2,1,0:T(8,128)(2,1)S(1)} async-done(((bf16[8,256,256]{2,1,0:T(8,128)(2,1)}), bf16[8,256,256]{2,1,0:T(8,128)(2,1)S(1)}, u32[]{:S(2)}, u32[]{:S(2)}) %all-to-all-start.4) | async-done | bytes 1048608 | tf_op jit(solution)/shard_map/all_to_all | solution.py:63
  311.7 53.5 %all_to_all.42.own_ref = bf16[8,256,1024]{2,1,0:T(8,128)(2,1)} all-to-all(bf16[8,256,1024]{2,1,0:T(8,128)(2,1)S(1)} %broadcast_in_dim.51), channel_id=1, replica_groups=mesh['patch'=16,'tensor'=8] {'tensor'}, dimensions={0} | all-to-all | bytes 8388608 | tf_op jit(solution)/shard_map/all_to_all | solution.py:63
  369.0 6.1 %collective-permute-done.22.refs_1_ = bf16[256,512]{1,0:T(8,128)(2,1)S(1)} collective-permute-done((bf16[256,512]{1,0:T(8,128)(2,1)S(1)}, bf16[256,512]{1,0:T(8,128)(2,1)S(1)}, u32[]{:S(2)}, u32[]{:S(2)}) %collective-permute-start.22) | collective-permute-done | bytes 262176 | tf_op jit(solution)/shard_map/ppermute | solution.py:45
  376.3 6.4 %collective-permute-done.27 = bf16[128,512]{1,0:T(8,128)(2,1)S(1)} collective-permute-done((bf16[128,512]{1,0:T(8,128)(2,1)S(1)}, bf16[128,512]{1,0:T(8,128)(2,1)S(1)}, u32[]{:S(2)}, u32[]{:S(2)}) %collective-permute-start.27) | collective-permute-done | bytes 131104 | tf_op jit(solution)/shard_map/ppermute | solution.py:45
  382.7 5.0 %collective-permute-done.28 = bf16[128,512]{1,0:T(8,128)(2,1)S(1)} collective-permute-done((bf16[128,512]{1,0:T(8,128)(2,1)S(1)}, bf16[128,512]{1,0:T(8,128)(2,1)S(1)}, u32[]{:S(2)}, u32[]{:S(2)}) %collective-permute-start.28) | collective-permute-done | bytes 131104 | tf_op jit(solution)/shard_map/ppermute | solution.py:45
  392.4 5.3 %collective-permute-done.29.refs_7_ = bf16[256,512]{1,0:T(8,128)(2,1)} collective-permute-done((bf16[256,512]{1,0:T(8,128)(2,1)S(1)}, bf16[256,512]{1,0:T(8,128)(2,1)}, u32[]{:S(2)}, u32[]{:S(2)}) %collective-permute-start.29) | collective-permute-done | bytes 262176 | tf_op jit(solution)/shard_map/ppermute | solution.py:45
  405.4 4.4 shard_map.190
  409.8 20.2 %all_to_all.43.att_ref = bf16[8,256,256]{2,1,0:T(8,128)(2,1)S(1)} all-to-all(bf16[8,256,256]{2,1,0:T(8,128)(2,1)S(1)} %broadcast_in_dim.52), channel_id=1, replica_groups=mesh['patch'=16,'tensor'=8] {'tensor'}, dimensions={0} | all-to-all | bytes 2097152 | tf_op jit(solution)/shard_map/all_to_all | solution.py:63
  430.0 14.1 %shard_map.191 = (bf16[8,256,256]{2,1,0:T(8,128)(2,1)}, f32[256,256]{1,0:T(8,128)S(1)}) custom-call(s32[2]{0:T(128)S(1)} %pad_add_fusion.ids, bf16[8,256,256]{2,1,0:T(8,128)(2,1)S(1)} %all_to_all.43.att_ref, bf16[8,256,256]{2,1,0:T(8,128)(2,1)S(1)} %all-to-all-done.4.emb_ref, bf16[8,256,1024]{2,1,0:T(8,128)(2,1)} %all_to_all.42.own_ref, ...), custom_call_target="tpu_custom_call" | custom-call | flops 6442450944 | bytes 23076872 | tf_op jit(solution)/shard_map/pallas_call | solution.py:90
  444.2 3.6 all-to-all-start.7
  448.4 15.8 %all-to-all-done.7 = bf16[8,256,256]{2,1,0:T(8,128)(2,1)S(1)} async-done(((bf16[8,256,256]{2,1,0:T(8,128)(2,1)}), bf16[8,256,256]{2,1,0:T(8,128)(2,1)S(1)}, u32[]{:S(2)}, u32[]{:S(2)}) %all-to-all-start.7) | async-done | bytes 1048608 | tf_op jit(solution)/shard_map/all_to_all | solution.py:63
  (203 shorter events, 76.2 us)
Async XLA Ops:
  76.3 58.2 %collective-permute-start.10 = (f32[8,128,896]{2,1,0:T(8,128)}, f32[8,128,896]{2,1,0:T(8,128)}, u32[]{:S(2)}, u32[]{:S(2)}) collective-permute-start(f32[8,128,896]{2,1,0:T(8,128)} %all_to_all.40.own_ref), channel_id=1, source_target_pairs={{0,8},{8,0},{16,24},{24,16},{32,40},{40,32},{48,56},{56,48},{64,72... | collective-permute-start | bytes 11010056 | tf_op jit(solution)/shard_map/ppermute | solution.py:45
  76.4 10.0 %collective-permute-start.5 = (f32[512,128]{1,0:T(8,128)S(1)}, f32[512,128]{1,0:T(8,128)S(1)}, u32[]{:S(2)}, u32[]{:S(2)}) collective-permute-start(f32[512,128]{1,0:T(8,128)S(1)} %pad_maximum_fusion.3.refs_0_), channel_id=1, source_target_pairs={{0,32},{8,40},{16,48},{24,56},{32,64},{40,72},{48,80},{56,88},{64,... | collective-permute-start | bytes 786440 | tf_op jit(solution)/shard_map/ppermute | solution.py:45
  77.9 8.8 %collective-permute-start.3 = (f32[512,128]{1,0:T(8,128)S(1)}, f32[512,128]{1,0:T(8,128)S(1)}, u32[]{:S(2)}, u32[]{:S(2)}) collective-permute-start(f32[512,128]{1,0:T(8,128)S(1)} %pad_maximum_fusion.3.refs_0_), channel_id=1, source_target_pairs={{0,96},{8,104},{16,112},{24,120},{32,0},{40,8},{48,16},{56,24},{64... | collective-permute-start | bytes 786440 | tf_op jit(solution)/shard_map/ppermute | solution.py:45
  79.6 10.9 %collective-permute-start.1 = (f32[512,128]{1,0:T(8,128)S(1)}, f32[512,128]{1,0:T(8,128)S(1)}, u32[]{:S(2)}, u32[]{:S(2)}) collective-permute-start(f32[512,128]{1,0:T(8,128)S(1)} %pad_maximum_fusion.3.refs_0_), channel_id=1, source_target_pairs={{0,16},{8,24},{16,0},{24,8},{32,48},{40,56},{48,32},{56,40},{64,80... | collective-permute-start | bytes 786440 | tf_op jit(solution)/shard_map/ppermute | solution.py:45
  86.4 6.4 %collective-permute-start.6 = (f32[256,128]{1,0:T(8,128)S(1)}, f32[256,128]{1,0:T(8,128)S(1)}, u32[]{:S(2)}, u32[]{:S(2)}) collective-permute-start(f32[256,128]{1,0:T(8,128)S(1)} %slice.132), channel_id=1, source_target_pairs={{0,32},{8,40},{16,48},{24,56},{32,64},{40,72},{48,80},{56,88},{64,... | collective-permute-start | bytes 393224 | tf_op jit(solution)/shard_map/ppermute | solution.py:45
  89.8 9.3 %collective-permute-start.4 = (f32[512,128]{1,0:T(8,128)S(1)}, f32[512,128]{1,0:T(8,128)S(1)}, u32[]{:S(2)}, u32[]{:S(2)}) collective-permute-start(f32[512,128]{1,0:T(8,128)S(1)} %collective-permute-done.3.refs_2_), channel_id=1, source_target_pairs={{0,16},{8,24},{16,0},{24,8},{32,48},{40,56},{48,32},{56,40},{64,80... | collective-permute-start | bytes 786440 | tf_op jit(solution)/shard_map/ppermute | solution.py:45
  90.5 8.3 %collective-permute-start.2 = (f32[512,128]{1,0:T(8,128)S(1)}, f32[512,128]{1,0:T(8,128)S(1)}, u32[]{:S(2)}, u32[]{:S(2)}) collective-permute-start(f32[512,128]{1,0:T(8,128)S(1)} %collective-permute-done.1.refs_3_), channel_id=1, source_target_pairs={{0,32},{8,40},{16,48},{24,56},{32,64},{40,72},{48,80},{56,88},{64,... | collective-permute-start | bytes 786440 | tf_op jit(solution)/shard_map/ppermute | solution.py:45
  92.8 10.1 %collective-permute-start.8 = (f32[512,128]{1,0:T(8,128)S(1)}, f32[512,128]{1,0:T(8,128)S(1)}, u32[]{:S(2)}, u32[]{:S(2)}) collective-permute-start(f32[512,128]{1,0:T(8,128)S(1)} %constant_dynamic-update-slice_fusion.refs_2_), channel_id=1, source_target_pairs={{0,16},{8,24},{16,0},{24,8},{32,48},{40,56},{48,32},{56,40},{64,80... | collective-permute-start | bytes 786440 | tf_op jit(solution)/shard_map/ppermute | solution.py:45
  112.5 22.1 %all-to-all-start.1 = ((f32[8,256,128]{2,1,0:T(8,128)}), f32[8,256,128]{2,1,0:T(8,128)}, u32[]{:S(2)}, u32[]{:S(2)}) async-start(f32[8,256,128]{2,1,0:T(8,128)} %broadcast_in_dim.42), calls=%async_computation.1 | async-start | bytes 2097152 | tf_op jit(solution)/shard_map/all_to_all | solution.py:63
  214.1 57.6 %collective-permute-start.21 = (f32[8,128,896]{2,1,0:T(8,128)}, f32[8,128,896]{2,1,0:T(8,128)}, u32[]{:S(2)}, u32[]{:S(2)}) collective-permute-start(f32[8,128,896]{2,1,0:T(8,128)} %all_to_all.41.own_ref), channel_id=1, source_target_pairs={{0,8},{8,0},{16,24},{24,16},{32,40},{40,32},{48,56},{56,48},{64,72... | collective-permute-start | bytes 11010056 | tf_op jit(solution)/shard_map/ppermute | solution.py:45
  214.1 9.9 %collective-permute-start.16 = (f32[512,128]{1,0:T(8,128)S(1)}, f32[512,128]{1,0:T(8,128)S(1)}, u32[]{:S(2)}, u32[]{:S(2)}) collective-permute-start(f32[512,128]{1,0:T(8,128)S(1)} %pad_maximum_fusion.5.refs_0_), channel_id=1, source_target_pairs={{0,32},{8,40},{16,48},{24,56},{32,64},{40,72},{48,80},{56,88},{64,... | collective-permute-start | bytes 786440 | tf_op jit(solution)/shard_map/ppermute | solution.py:45
  214.1 10.0 %collective-permute-start.14 = (f32[512,128]{1,0:T(8,128)S(1)}, f32[512,128]{1,0:T(8,128)S(1)}, u32[]{:S(2)}, u32[]{:S(2)}) collective-permute-start(f32[512,128]{1,0:T(8,128)S(1)} %pad_maximum_fusion.5.refs_0_), channel_id=1, source_target_pairs={{0,96},{8,104},{16,112},{24,120},{32,0},{40,8},{48,16},{56,24},{64... | collective-permute-start | bytes 786440 | tf_op jit(solution)/shard_map/ppermute | solution.py:45
  217.4 10.8 %collective-permute-start.12 = (f32[512,128]{1,0:T(8,128)S(1)}, f32[512,128]{1,0:T(8,128)S(1)}, u32[]{:S(2)}, u32[]{:S(2)}) collective-permute-start(f32[512,128]{1,0:T(8,128)S(1)} %pad_maximum_fusion.5.refs_0_), channel_id=1, source_target_pairs={{0,16},{8,24},{16,0},{24,8},{32,48},{40,56},{48,32},{56,40},{64,80... | collective-permute-start | bytes 786440 | tf_op jit(solution)/shard_map/ppermute | solution.py:45
  224.1 6.3 %collective-permute-start.17 = (f32[256,128]{1,0:T(8,128)S(1)}, f32[256,128]{1,0:T(8,128)S(1)}, u32[]{:S(2)}, u32[]{:S(2)}) collective-permute-start(f32[256,128]{1,0:T(8,128)S(1)} %slice.138), channel_id=1, source_target_pairs={{0,32},{8,40},{16,48},{24,56},{32,64},{40,72},{48,80},{56,88},{64,... | collective-permute-start | bytes 393224 | tf_op jit(solution)/shard_map/ppermute | solution.py:45
  224.2 6.2 %collective-permute-start.18 = (f32[256,128]{1,0:T(8,128)S(1)}, f32[256,128]{1,0:T(8,128)S(1)}, u32[]{:S(2)}, u32[]{:S(2)}) collective-permute-start(f32[256,128]{1,0:T(8,128)S(1)} %slice.139), channel_id=1, source_target_pairs={{0,96},{8,104},{16,112},{24,120},{32,0},{40,8},{48,16},{56,24},{64... | collective-permute-start | bytes 393224 | tf_op jit(solution)/shard_map/ppermute | solution.py:45
  227.5 9.3 %collective-permute-start.15 = (f32[512,128]{1,0:T(8,128)S(1)}, f32[512,128]{1,0:T(8,128)S(1)}, u32[]{:S(2)}, u32[]{:S(2)}) collective-permute-start(f32[512,128]{1,0:T(8,128)S(1)} %collective-permute-done.14.refs_2_), channel_id=1, source_target_pairs={{0,16},{8,24},{16,0},{24,8},{32,48},{40,56},{48,32},{56,40},{64,80... | collective-permute-start | bytes 786440 | tf_op jit(solution)/shard_map/ppermute | solution.py:45
  228.2 8.2 %collective-permute-start.13 = (f32[512,128]{1,0:T(8,128)S(1)}, f32[512,128]{1,0:T(8,128)S(1)}, u32[]{:S(2)}, u32[]{:S(2)}) collective-permute-start(f32[512,128]{1,0:T(8,128)S(1)} %collective-permute-done.12.refs_3_), channel_id=1, source_target_pairs={{0,32},{8,40},{16,48},{24,56},{32,64},{40,72},{48,80},{56,88},{64,... | collective-permute-start | bytes 786440 | tf_op jit(solution)/shard_map/ppermute | solution.py:45
  230.5 10.1 %collective-permute-start.19 = (f32[512,128]{1,0:T(8,128)S(1)}, f32[512,128]{1,0:T(8,128)S(1)}, u32[]{:S(2)}, u32[]{:S(2)}) collective-permute-start(f32[512,128]{1,0:T(8,128)S(1)} %constant_dynamic-update-slice_fusion.2.refs_2_), channel_id=1, source_target_pairs={{0,16},{8,24},{16,0},{24,8},{32,48},{40,56},{48,32},{56,40},{64,80... | collective-permute-start | bytes 786440 | tf_op jit(solution)/shard_map/ppermute | solution.py:45
  250.2 21.5 %all-to-all-start.3 = ((f32[8,256,128]{2,1,0:T(8,128)}), f32[8,256,128]{2,1,0:T(8,128)S(1)}, u32[]{:S(2)}, u32[]{:S(2)}) async-start(f32[8,256,128]{2,1,0:T(8,128)} %broadcast_in_dim.45), calls=%async_computation.3 | async-start | bytes 2097152 | tf_op jit(solution)/shard_map/all_to_all | solution.py:63
  288.0 20.4 %all-to-all-start.4 = ((bf16[8,256,256]{2,1,0:T(8,128)(2,1)}), bf16[8,256,256]{2,1,0:T(8,128)(2,1)S(1)}, u32[]{:S(2)}, u32[]{:S(2)}) async-start(bf16[8,256,256]{2,1,0:T(8,128)(2,1)} %broadcast_in_dim.47), calls=%async_computation.4 | async-start | bytes 2097152 | tf_op jit(solution)/shard_map/all_to_all | solution.py:63
  365.1 64.9 %collective-permute-start.38 = (bf16[8,256,1024]{2,1,0:T(8,128)(2,1)}, bf16[8,256,1024]{2,1,0:T(8,128)(2,1)}, u32[]{:S(2)}, u32[]{:S(2)}) collective-permute-start(bf16[8,256,1024]{2,1,0:T(8,128)(2,1)} %all_to_all.42.own_ref), channel_id=1, source_target_pairs={{0,8},{8,0},{16,24},{24,16},{32,40},{40,32},{48,56},{56,48},{64,72... | collective-permute-start | bytes 12582920 | tf_op jit(solution)/shard_map/ppermute | solution.py:45
  365.1 9.9 %collective-permute-start.22 = (bf16[256,512]{1,0:T(8,128)(2,1)S(1)}, bf16[256,512]{1,0:T(8,128)(2,1)S(1)}, u32[]{:S(2)}, u32[]{:S(2)}) collective-permute-start(bf16[256,512]{1,0:T(8,128)(2,1)S(1)} %get-tuple-element.51.refs_0_), channel_id=1, source_target_pairs={{0,32},{8,40},{16,48},{24,56},{32,64},{40,72},{48,80},{56,88},{64,... | collective-permute-start | bytes 786440 | tf_op jit(solution)/shard_map/ppermute | solution.py:45
  365.1 10.4 %collective-permute-start.24 = (bf16[256,512]{1,0:T(8,128)(2,1)S(1)}, bf16[256,512]{1,0:T(8,128)(2,1)S(1)}, u32[]{:S(2)}, u32[]{:S(2)}) collective-permute-start(bf16[256,512]{1,0:T(8,128)(2,1)S(1)} %get-tuple-element.51.refs_0_), channel_id=1, source_target_pairs={{0,16},{8,24},{16,0},{24,8},{32,48},{40,56},{48,32},{56,40},{64,80... | collective-permute-start | bytes 786440 | tf_op jit(solution)/shard_map/ppermute | solution.py:45
  365.7 9.9 %collective-permute-start.23 = (bf16[256,512]{1,0:T(8,128)(2,1)S(1)}, bf16[256,512]{1,0:T(8,128)(2,1)S(1)}, u32[]{:S(2)}, u32[]{:S(2)}) collective-permute-start(bf16[256,512]{1,0:T(8,128)(2,1)S(1)} %get-tuple-element.51.refs_0_), channel_id=1, source_target_pairs={{0,96},{8,104},{16,112},{24,120},{32,0},{40,8},{48,16},{56,24},{64... | collective-permute-start | bytes 786440 | tf_op jit(solution)/shard_map/ppermute | solution.py:45
  375.1 7.6 %collective-permute-start.27 = (bf16[128,512]{1,0:T(8,128)(2,1)S(1)}, bf16[128,512]{1,0:T(8,128)(2,1)S(1)}, u32[]{:S(2)}, u32[]{:S(2)}) collective-permute-start(bf16[128,512]{1,0:T(8,128)(2,1)S(1)} %slice.142), channel_id=1, source_target_pairs={{0,32},{8,40},{16,48},{24,56},{32,64},{40,72},{48,80},{56,88},{64,... | collective-permute-start | bytes 393224 | tf_op jit(solution)/shard_map/ppermute | solution.py:45
  375.2 12.5 %collective-permute-start.30 = (bf16[256,512]{1,0:T(8,128)(2,1)S(1)}, bf16[256,512]{1,0:T(8,128)(2,1)S(1)}, u32[]{:S(2)}, u32[]{:S(2)}) collective-permute-start(bf16[256,512]{1,0:T(8,128)(2,1)S(1)} %get-tuple-element.51.refs_0_), channel_id=1, source_target_pairs={{0,8},{8,0},{16,24},{24,16},{32,40},{40,32},{48,56},{56,48},{64,72... | collective-permute-start | bytes 786440 | tf_op jit(solution)/shard_map/ppermute | solution.py:45
  375.5 13.4 %collective-permute-start.25 = (bf16[256,512]{1,0:T(8,128)(2,1)S(1)}, bf16[256,512]{1,0:T(8,128)(2,1)}, u32[]{:S(2)}, u32[]{:S(2)}) collective-permute-start(bf16[256,512]{1,0:T(8,128)(2,1)S(1)} %collective-permute-done.24.refs_3_), channel_id=1, source_target_pairs={{0,32},{8,40},{16,48},{24,56},{32,64},{40,72},{48,80},{56,88},{64,... | collective-permute-start | bytes 786440 | tf_op jit(solution)/shard_map/ppermute | solution.py:45
  375.6 13.3 %collective-permute-start.26 = (bf16[256,512]{1,0:T(8,128)(2,1)S(1)}, bf16[256,512]{1,0:T(8,128)(2,1)}, u32[]{:S(2)}, u32[]{:S(2)}) collective-permute-start(bf16[256,512]{1,0:T(8,128)(2,1)S(1)} %collective-permute-done.23.refs_2_), channel_id=1, source_target_pairs={{0,16},{8,24},{16,0},{24,8},{32,48},{40,56},{48,32},{56,40},{64,80... | collective-permute-start | bytes 786440 | tf_op jit(solution)/shard_map/ppermute | solution.py:45
  389.0 8.8 %collective-permute-start.29 = (bf16[256,512]{1,0:T(8,128)(2,1)S(1)}, bf16[256,512]{1,0:T(8,128)(2,1)}, u32[]{:S(2)}, u32[]{:S(2)}) collective-permute-start(bf16[256,512]{1,0:T(8,128)(2,1)S(1)} %constant_dynamic-update-slice_fusion.4.refs_6_), channel_id=1, source_target_pairs={{0,16},{8,24},{16,0},{24,8},{32,48},{40,56},{48,32},{56,40},{64,80... | collective-permute-start | bytes 786440 | tf_op jit(solution)/shard_map/ppermute | solution.py:45
  390.3 7.7 %collective-permute-start.36 = (bf16[256,512]{1,0:T(8,128)(2,1)S(1)}, bf16[256,512]{1,0:T(8,128)(2,1)}, u32[]{:S(2)}, u32[]{:S(2)}) collective-permute-start(bf16[256,512]{1,0:T(8,128)(2,1)S(1)} %constant_dynamic-update-slice_fusion.4.refs_6_), channel_id=1, source_target_pairs={{0,8},{8,0},{16,24},{24,16},{32,40},{40,32},{48,56},{56,48},{64,72... | collective-permute-start | bytes 786440 | tf_op jit(solution)/shard_map/ppermute | solution.py:45
  391.2 6.8 %collective-permute-start.34 = (bf16[256,512]{1,0:T(8,128)(2,1)}, bf16[256,512]{1,0:T(8,128)(2,1)}, u32[]{:S(2)}, u32[]{:S(2)}) collective-permute-start(bf16[256,512]{1,0:T(8,128)(2,1)} %collective-permute-done.25.refs_4_), channel_id=1, source_target_pairs={{0,8},{8,0},{16,24},{24,16},{32,40},{40,32},{48,56},{56,48},{64,72... | collective-permute-start | bytes 786440 | tf_op jit(solution)/shard_map/ppermute | solution.py:45
  444.2 20.0 %all-to-all-start.7 = ((bf16[8,256,256]{2,1,0:T(8,128)(2,1)}), bf16[8,256,256]{2,1,0:T(8,128)(2,1)S(1)}, u32[]{:S(2)}, u32[]{:S(2)}) async-start(bf16[8,256,256]{2,1,0:T(8,128)(2,1)} %get-tuple-element.54), calls=%async_computation.7 | async-start | bytes 2097152 | tf_op jit(solution)/shard_map/all_to_all | solution.py:63
  (48 other events, 720.8 us)
where the time goes:
time: 473 us; the launch traced here: 465 us
  blocking collectives  177 us (37%)
  waiting for transfers between devices  117 us (25%)
  Pallas kernels  85.6 us (18%)
  local copies, waits for them, and re-layouts  43 us (9%)
  starting transfers between devices  39.6 us (8%)
    all_to_all x4, blocking collectives, exchange(): return lax.all_to_all(parts, 'tensor', 0, 0)  177 us
    pallas_call x7, Pallas kernels, call(): pl.pallas_call(body, in_specs=[SMEM] * smem + [VMEM] * (len(args) - smem)...  63.3 us
    all_to_all x4, waiting for transfers between devices, exchange(): return lax.all_to_all(parts, 'tensor', 0, 0)  61.2 us
    ppermute x39, waiting for transfers between devices, over(): return lax.ppermute(value, 'patch', pairs)  55.4 us
    ppermute x39, starting transfers between devices, over(): return lax.ppermute(value, 'patch', pairs)  24.5 us
    unnamed x79, local copies, waits for them, and re-layouts  23.3 us
    pallas_call x4, Pallas kernels, attend(): pl.pallas_call(functools.partial(attend_kernel, count, not state, last),...  22.3 us
    all_to_all x4, starting transfers between devices, exchange(): return lax.all_to_all(parts, 'tensor', 0, 0)  15.1 us
  transfers between devices with their start and end apart: 43, of which 22 were waited for; matrix products, arithmetic and copies ran while one was open for 3% of the time, Pallas kernels for 6%

commit v1 on v0

--- a/solution.py
+++ b/solution.py
@@ -14,17 +14,12 @@
 NT = 8
 
 
-highest = lax.Precision.HIGHEST
 bf16 = jnp.bfloat16
 f32 = jnp.float32
 
 
 def normed(value, gain):
     return value * lax.rsqrt(jnp.mean(value * value, axis=-1, keepdims=True) + 1e-06) * gain
-
-
-def mm32(left, right):
-    return jnp.dot(left, right, precision=highest, preferred_element_type=f32)
 
 
 CORE = [(i, i ^ 1) for i in range(NP)]
@@ -63,6 +58,16 @@
     return lax.all_to_all(parts, "tensor", 0, 0)
 
 
+ACROSS = [(i, i ^ 1) for i in range(NT)]
+COLUMNS = [[2 * z + x for z in range(NT // 2)] for x in range(2)]
+
+
+def spread(own, side):
+    pair = jnp.stack([own, side])
+    parts = jnp.broadcast_to(pair, (NT // 2,) + pair.shape)
+    return lax.all_to_all(parts, "tensor", 0, 0, axis_index_groups=COLUMNS)
+
+
 def split2(x):
     a = x.astype(bf16)
     b = (x - a.astype(f32)).astype(bf16)
@@ -77,15 +82,54 @@
     return a, b, c
 
 
-def select(x, one_hot):
-    return sum(jnp.dot(p, one_hot, preferred_element_type=f32) for p in reversed(split3(x)))
+def select(x, one_hot, dims=(1, 0)):
+    dims = (((dims[0],), (dims[1],)), ((), ()))
+    a, b, c = (
+        lax.dot_general(p, one_hot, dims, preferred_element_type=f32) for p in split3(x)
+    )
+    return (c + b) + a
+
+
+def left6(x):
+    a, b, c = split3(x)
+    return jnp.concatenate([a, a, b, a, b, c], axis=1)
+
+
+def right6(x):
+    a, b, c = split3(x)
+    return jnp.concatenate([a, b, a, c, b, a], axis=0)
+
+
+def left3(x):
+    a, b = split2(x)
+    return jnp.concatenate([a, a, b], axis=1)
+
+
+def right3(x):
+    a, b = split2(x)
+    return jnp.concatenate([a, b, a], axis=0)
+
+
+def dot(left, right):
+    return jnp.dot(left, right, preferred_element_type=f32)
+
+
+TILE = 256
+
+
+def tiles(count, body):
+    def step(i, carry):
+        body(pl.multiple_of(i * TILE, TILE))
+        return carry
+
+    lax.fori_loop(0, count, step, 0)
 
 
 VMEM = pl.BlockSpec(memory_space=pltpu.VMEM)
 SMEM = pl.BlockSpec(memory_space=pltpu.SMEM)
 
 
-def call(body, outs, *args, scratch=(), flops=0, limit=40, smem=0):
+def call(body, outs, *args, scratch=(), flops=0, limit=16, smem=0):
     moved = sum(x.size * x.dtype.itemsize for x in args)
     return pl.pallas_call(
         body,
@@ -98,43 +142,83 @@
     )(*args)
 
 
-def pre_kernel(ids, field_ref, perm_ref, w_in_ref, gain_ref, w_ref, hidden_ref, q_ref, kv_ref, oth_ref):
+def cut_kernel(ids, mix_ref, head_ref, *refs):
+    outs, sems = refs[:BLOCKS], refs[BLOCKS]
+    copies = []
+    for blk, out in enumerate(outs):
+        at = 0
+        for i, ref in enumerate((mix_ref, head_ref)):
+            cols = ref.shape[2] // 2
+            source = ref.at[blk, :, pl.ds(pl.multiple_of(ids[0] * cols, 128), cols)]
+            copies.append(
+                pltpu.make_async_copy(source, out.at[:, at : at + cols], sems.at[blk, i])
+            )
+            at += cols
+    for copy in copies:
+        copy.start()
+    for copy in copies:
+        copy.wait()
+
+
+def cut(ids, w_mix, w_head):
+    shape = (w_mix.shape[1], (w_mix.shape[2] + w_head.shape[2]) // 2)
+    hbm = pl.BlockSpec(memory_space=pl.ANY)
+    return pl.pallas_call(
+        cut_kernel,
+        in_specs=[SMEM, hbm, hbm],
+        out_specs=[VMEM] * BLOCKS,
+        out_shape=[jax.ShapeDtypeStruct(shape, f32)] * BLOCKS,
+        scratch_shapes=[pltpu.SemaphoreType.DMA((BLOCKS, 2))],
+        compiler_params=pltpu.CompilerParams(vmem_limit_bytes=4 << 20),
+        name="cut",
+    )(ids, w_mix, w_head)
+
+
+def pre_kernel(
+    blk, ids, field_ref, perms_ref, w_in_ref, gain_ref, w_ref,
+    hidden_ref, q_ref, kv_ref, oth_ref, cond_ref, unit_ref,
+):
     even = ids[0] == 0
-    half = w_in_ref.shape[0]
+    half, full = w_in_ref.shape[1:]
     width = field_ref.shape[1]
-    lanes = w_ref.shape[1] // 3
-    hd = lanes // 2
+    hd = w_ref.shape[3] // 2
     row = lax.broadcasted_iota(jnp.int32, (width, half), 0)
-    take = jnp.where(row == perm_ref[...], 1.0, 0.0).astype(bf16)
-    cond = select(field_ref[...], take)
-    hidden = mm32(cond, w_in_ref[...])
-    hidden_ref[...] = hidden
-    unit = normed(hidden, gain_ref[...])
-    qkv = mm32(unit, w_ref[...])
-
-    def pick(i, first):
-        x = qkv[:, i * lanes : (i + 1) * lanes]
+    take = jnp.where(row == perms_ref[blk : blk + 1, :half], 1.0, 0.0).astype(bf16)
+    cond_ref[...] = left6(select(field_ref[...], take))
+
+    def column(at):
+        cut = pl.ds(at, TILE)
+        hidden_ref[:, cut] = dot(cond_ref[...], right6(w_in_ref[blk, :, cut]))
+
+    tiles(full // TILE, column)
+    unit_ref[...] = left6(normed(hidden_ref[...], gain_ref[blk : blk + 1]))
+    qk = jnp.concatenate([w_ref[blk, 0], w_ref[blk, 1]], axis=1)
+    qk = dot(unit_ref[...], right6(qk))
+    v = dot(unit_ref[...], right6(w_ref[blk, 2]))
+    q, k = qk[:, : 2 * hd], qk[:, 2 * hd :]
+
+    def pick(x, first):
         return jnp.where(first, x[:, :hd], x[:, hd:])
 
-    q_ref[...] = pick(0, even)
-    kv_ref[...] = jnp.concatenate([pick(1, even), pick(2, even)], axis=1)
+    q_ref[...] = pick(q, even)
+    kv_ref[...] = jnp.concatenate([pick(k, even), pick(v, even)], axis=1)
     odd = jnp.logical_not(even)
-    oth_ref[...] = jnp.concatenate([pick(0, odd), pick(1, odd), pick(2, odd)], axis=1)
-
-
-def pre(ids, field, perm, w_in, gain, w_qkv):
-    rows, full = field.shape[0], w_in.shape[1]
-    lanes = w_qkv.shape[1] // 3
-    hd = lanes // 2
+    oth_ref[...] = jnp.concatenate([pick(q, odd), pick(k, odd), pick(v, odd)], axis=1)
+
+
+def pre(blk, ids, field, perms, w_in, gain, w_qkv):
+    rows, (half, full) = field.shape[0], w_in.shape[1:]
+    hd = w_qkv.shape[3] // 2
     return call(
-        pre_kernel,
+        functools.partial(pre_kernel, blk),
         [((rows, full), f32), ((rows, hd), f32), ((rows, 2 * hd), f32), ((rows, 3 * hd), f32)],
         ids,
         field,
-        perm[None, : w_in.shape[0]],
+        perms,
         w_in,
-        gain[None],
+        gain,
         w_qkv,
+        scratch=[pltpu.VMEM((rows, 6 * half), bf16), pltpu.VMEM((rows, 6 * full), bf16)],
         smem=1,
         flops=3 << 30,
     )
@@ -198,7 +282,7 @@
         out_specs=[by_rows(w) for w in widths],
         out_shape=[jax.ShapeDtypeStruct((rows, w), f32) for w in widths],
         scratch_shapes=[pltpu.VMEM((count, block, keys), f32)],
-        compiler_params=pltpu.CompilerParams(vmem_limit_bytes=32 << 20),
+        compiler_params=pltpu.CompilerParams(vmem_limit_bytes=16 << 20),
         cost_estimate=pl.CostEstimate(
             flops=4 << 30, bytes_accessed=count * keys * hd * 8, transcendentals=rows * keys * count
         ),
@@ -206,41 +290,54 @@
     )(query, *pieces, *state)
 
 
-def post_kernel(ids, m_ref, own_ref, oth_ref, hidden_ref, field_ref, perm_ref, gain_ref, out_ref, det_ref):
+def post_kernel(
+    blk, ids, m_ref, own_ref, oth_ref, hidden_ref, field_ref, perms_ref, gain_ref,
+    out_ref, det_ref, left_ref, sum_ref,
+):
     even = ids[0] == 0
     nt, _, lanes = m_ref.shape
     full, width = hidden_ref.shape[1], field_ref.shape[1]
     half, mid = width // 2, full // 2
-    mixed = jnp.concatenate([m_ref[t] for t in range(nt)], axis=1)
-
-    def product(left, lo, hi):
-        a = mm32(left, own_ref[:, :, lo:hi].reshape(nt * lanes, hi - lo))
-        b = mm32(left, oth_ref[:, :, lo:hi].reshape(nt * lanes, hi - lo))
-        return jnp.where(even, a, b), jnp.where(even, b, a)
-
-    hidden = hidden_ref[...] + jnp.concatenate(product(mixed, 0, mid), axis=1)
-    raw, shift = product(normed(hidden, gain_ref[...]), mid, mid + half)
-    log_scale = jnp.tanh(raw)
+    order = [2 * (t // 2) + (ids[1] + t) % 2 for t in range(nt)]
+    left_ref[...] = left3(jnp.concatenate([m_ref[t] for t in order], axis=1))
+
+    def column(at):
+        cut = pl.ds(at, TILE)
+        a = dot(left_ref[...], right3(own_ref[:, :, cut].reshape(full, TILE)))
+        b = dot(left_ref[...], right3(oth_ref[:, :, cut].reshape(full, TILE)))
+        sum_ref[:, cut] = hidden_ref[:, cut] + jnp.where(even, a, b)
+        cut = pl.ds(pl.multiple_of(at + mid, TILE), TILE)
+        sum_ref[:, cut] = hidden_ref[:, cut] + jnp.where(even, b, a)
+
+    tiles(mid // TILE, column)
+    sum_ref[...] = normed(sum_ref[...], gain_ref[blk : blk + 1])
+    parts = [sum_ref[:, pl.ds(pl.multiple_of(t * lanes, lanes), lanes)] for t in order]
+    left_ref[...] = left3(jnp.concatenate(parts, axis=1))
+    a = dot(left_ref[...], right3(own_ref[:, :, mid:].reshape(full, half)))
+    b = dot(left_ref[...], right3(oth_ref[:, :, mid:].reshape(full, half)))
+    log_scale, shift = jnp.tanh(jnp.where(even, a, b)), jnp.where(even, b, a)
     det_ref[...] = jnp.sum(log_scale, axis=1, keepdims=True)
-    col = lax.broadcasted_iota(jnp.int32, (half, width), 1)
-    put = jnp.where(col == perm_ref[...], 1.0, 0.0).astype(bf16)
-    field = field_ref[...] * jnp.exp(select(log_scale, put)) + select(shift, put)
+    row = lax.broadcasted_iota(jnp.int32, (width, half), 0)
+    put = jnp.where(row == perms_ref[blk : blk + 1, half:], 1.0, 0.0).astype(bf16)
+    field = field_ref[...] * jnp.exp(select(log_scale, put, (1, 1))) + select(shift, put, (1, 1))
     out_ref[...] = field.astype(out_ref.dtype)
 
 
-def post(ids, mixed, own, oth, hidden, field, perm, gain, kind):
+def post(blk, ids, mixed, own, oth, hidden, field, perms, gain, kind):
     rows, width = field.shape
+    full = hidden.shape[1]
     return call(
-        post_kernel,
+        functools.partial(post_kernel, blk),
         [((rows, width), kind), ((rows, 1), f32)],
         ids,
         mixed,
-        own,
-        oth,
+        own.reshape((NT,) + own.shape[2:]),
+        oth.reshape((NT,) + oth.shape[2:]),
         hidden,
         field,
-        perm[width // 2 :, None],
-        gain[None],
+        perms,
+        gain,
+        scratch=[pltpu.VMEM((rows, 3 * full), bf16), pltpu.VMEM((rows, full), f32)],
         smem=1,
         flops=6 << 30,
     )
@@ -283,31 +380,38 @@
 
 def mlp_kernel(
     ids, att_ref, emb_ref, own_ref, oth_ref, gain_ref, gate_ref, up_ref, down_ref,
-    out_ref, resid_ref, full_ref, inner_ref,
+    out_ref, resid_ref, full_ref, inner_ref, left_ref,
 ):
     even = ids[0] == 0
     nt, _, lanes = att_ref.shape
     half = own_ref.shape[2]
-    att = jnp.concatenate([att_ref[t] for t in range(nt)], axis=1)
-    tile = 256
-
-    for start in range(0, half, tile):
-        a = jnp.dot(att, own_ref[:, :, start : start + tile].reshape(-1, tile), preferred_element_type=f32)
-        b = jnp.dot(att, oth_ref[:, :, start : start + tile].reshape(-1, tile), preferred_element_type=f32)
-        for x, at in ((jnp.where(even, a, b), start), (jnp.where(even, b, a), half + start)):
-            full_ref[:, at : at + tile] = x + emb_ref[at // lanes].astype(f32)
-    mine = pl.multiple_of(ids[1] * lanes, lanes)
-    resid_ref[...] = full_ref[:, pl.ds(mine, lanes)]
-    unit = normed(full_ref[...], gain_ref[...]).astype(bf16)
-    for start in range(0, gate_ref.shape[1], tile):
-        cut = slice(start, start + tile)
-        gate = jnp.dot(unit, gate_ref[:, cut], preferred_element_type=f32)
-        up = jnp.dot(unit, up_ref[:, cut], preferred_element_type=f32)
+    order = [2 * (t // 2) + (ids[1] + t) % 2 for t in range(nt)]
+    left_ref[...] = jnp.concatenate([att_ref[t] for t in order], axis=1)
+
+    def project(at):
+        cut = pl.ds(at, TILE)
+        a = dot(left_ref[...], own_ref[:, :, cut].reshape(nt * lanes, TILE))
+        b = dot(left_ref[...], oth_ref[:, :, cut].reshape(nt * lanes, TILE))
+        full_ref[:, cut] = jnp.where(even, a, b) + emb_ref[at // lanes].astype(f32)
+        cut = pl.ds(pl.multiple_of(at + half, TILE), TILE)
+        full_ref[:, cut] = jnp.where(even, b, a) + emb_ref[(at + half) // lanes].astype(f32)
+
+    tiles(half // TILE, project)
+    resid_ref[...] = full_ref[:, pl.ds(pl.multiple_of(ids[1] * lanes, lanes), lanes)]
+    left_ref[...] = normed(full_ref[...], gain_ref[...]).astype(bf16)
+
+    def expand(at):
+        cut = pl.ds(at, TILE)
+        gate = dot(left_ref[...], gate_ref[:, cut])
+        up = dot(left_ref[...], up_ref[:, cut])
         inner_ref[:, cut] = (jax.nn.gelu(gate, approximate=True) * up).astype(bf16)
-    for t in range(nt):
-        out_ref[t] = jnp.dot(
-            inner_ref[...], down_ref[:, t * lanes : (t + 1) * lanes], preferred_element_type=f32
-        ).astype(bf16)
+
+    tiles(gate_ref.shape[1] // TILE, expand)
+
+    def contract(at):
+        out_ref[at // lanes] = dot(inner_ref[...], down_ref[:, pl.ds(at, TILE)]).astype(bf16)
+
+    tiles(nt * lanes // TILE, contract)
 
 
 def tied(value, *others):
@@ -335,7 +439,6 @@
     w_down,
 ):
     rows = patches.shape[0]
-    full = w_in.shape[2]
     local_w = w_qkv.shape[3]
     where = lax.axis_index("tensor")
     patch = lax.axis_index("patch")
@@ -347,21 +450,19 @@
         cols = x.shape[1] // 2
         return lax.dynamic_slice_in_dim(x, core * cols, cols, 1)
 
+    w_qkv = w_qkv.transpose(0, 2, 1, 3)
+    halved = cut(ids, w_mix, w_head)
+    own_weights = [halved[0], None]
+    side_weights = [lax.ppermute(halved[0], "tensor", ACROSS), None]
     field = patches
     logdet = 0.0
     for blk in range(BLOCKS):
-        perm = perms[blk]
-        hidden, query, keyval, other = pre(
-            ids, field, perm, w_in[blk], gain_mix[blk], w_qkv[blk].reshape(full, 3 * local_w)
-        )
+        hidden, query, keyval, other = pre(blk, ids, field, perms, w_in, gain_mix, w_qkv)
         hd = local_w // 2
         got = over(other, CORE)
         query = jnp.concatenate([query, got[:, :hd]], axis=0)
         keyval = jnp.concatenate([keyval, got[:, hd:]], axis=0)
-        weight = jnp.concatenate([halves(w_mix[blk]), halves(w_head[blk])], axis=1)
-        weight = tied(weight, keyval)
-        own_w = exchange(jnp.broadcast_to(weight, (NT,) + weight.shape))
-        oth_w = over(own_w, CORE)
+        own_w = spread(tied(own_weights[blk], keyval), side_weights[blk])
         pieces = gather_chips(keyval)
         state = attend(query, pieces[:4], [], False)
         (out,) = attend(query, pieces[4:], state, True)
@@ -371,9 +472,16 @@
             [jnp.where(even, front, back), jnp.where(even, back, front)], axis=1
         )
         mixed = tied(mixed, own_w)
+        oth_w = over(tied(own_w, mixed), CORE)
         mixed = exchange(jnp.broadcast_to(mixed, (NT,) + mixed.shape))
+        if blk + 1 < BLOCKS:
+            own_weights[blk + 1] = tied(halved[blk + 1], mixed)
+            side_weights[blk + 1] = lax.ppermute(own_weights[blk + 1], "tensor", ACROSS)
+        else:
+            attn_half = tied(halves(w_attn), mixed)
+            attn_side = lax.ppermute(attn_half, "tensor", ACROSS)
         field, det = post(
-            ids, mixed, own_w, oth_w, hidden, field, perm, gain_out[blk],
+            blk, ids, mixed, own_w, oth_w, hidden, field, perms, gain_out,
             bf16 if blk == BLOCKS - 1 else f32,
         )
         logdet = logdet + det[:, 0]
@@ -388,9 +496,7 @@
         w_keyval,
         flops=1 << 30,
     )
-    attn_half = tied(halves(w_attn), keyval)
-    own_a = exchange(jnp.broadcast_to(attn_half, (NT,) + attn_half.shape))
-    oth_a = over(own_a, CORE)
+    own_a = spread(tied(attn_half, keyval), attn_side)
     pieces = gather_chips(keyval)
     pieces = pieces + [over(x, CORE) for x in pieces]
 
@@ -412,6 +518,7 @@
         flops=2 << 30,
     )
     attended = tied(attended, own_a)
+    oth_a = over(tied(own_a, attended), CORE)
     att = exchange(jnp.broadcast_to(attended, (NT,) + attended.shape))
     cols = w_attn.shape[1] // NT
     down, resid = call(
@@ -420,8 +527,8 @@
         ids,
         att,
         embedded,
-        own_a,
-        oth_a,
+        own_a.reshape((NT,) + own_a.shape[2:]),
+        oth_a.reshape((NT,) + oth_a.shape[2:]),
         gain_mlp[None],
         w_gate,
         w_up,
@@ -429,6 +536,7 @@
         scratch=[
             pltpu.VMEM((rows, w_attn.shape[1]), f32),
             pltpu.VMEM((rows, w_gate.shape[1]), bf16),
+            pltpu.VMEM((rows, w_attn.shape[1]), bf16),
         ],
         smem=1,
         flops=6 << 30,

time: 473 us -> 351 us (0.74)
  blocking collectives: 177 us -> 63.4 us
  starting transfers between devices: 39.6 us -> 59.9 us
  Pallas kernels: 85.6 us -> 69.6 us
  waiting for transfers between devices: 117 us -> 110 us
  local copies, waits for them, and re-layouts: 43 us -> 36.1 us
    all_to_all x4 -> x3, blocking collectives: 177 us -> 63.4 us  [exchange(): return lax.all_to_all(parts, 'tensor', 0, 0)]
    all_to_all x4 -> x2, waiting for transfers between devices: 61.2 us -> 30.4 us  [exchange(): return lax.all_to_all(parts, 'tensor', 0, 0)]
    all_to_all x0 -> x3, waiting for transfers between devices: none -> 29.4 us  [spread(): return lax.all_to_all(parts, 'tensor', 0, 0, axis_index_groups=COLUMNS)]
    pallas_call x7, Pallas kernels: 63.3 us -> 46.4 us  [call(): pl.pallas_call(body, in_specs=[SMEM] * smem + [VMEM] * (len(args) - smem)...]
    all_to_all x0 -> x3, starting transfers between devices: none -> 15 us  [spread(): return lax.all_to_all(parts, 'tensor', 0, 0, axis_index_groups=COLUMNS)]
    ppermute x39, waiting for transfers between devices: 55.4 us -> 45.7 us  [over(): return lax.ppermute(value, 'patch', pairs)]
    all_to_all x4 -> x2, starting transfers between devices: 15.1 us -> 7.11 us  [exchange(): return lax.all_to_all(parts, 'tensor', 0, 0)]
    ppermute x0 -> x3, starting transfers between devices: none -> 7.85 us  [the longest x1 3.63 us: on_device(): attn_side = lax.ppermute(attn_half, 'tensor', ACROSS)]
  transfers between devices with their start and end apart: 43 -> 47, of which waited for: 22 -> 26; matrix products, arithmetic and copies ran while one was open for 3% -> 1% of each run, Pallas kernels for 6% -> 14%
where the time goes in v1:
time: 351 us; the launch traced here: 344 us
  waiting for transfers between devices  110 us (31%)
  Pallas kernels  69.6 us (20%)
  blocking collectives  63.4 us (18%)
  starting transfers between devices  59.9 us (17%)
  local copies, waits for them, and re-layouts  36.1 us (10%)
    all_to_all x3, blocking collectives, exchange(): return lax.all_to_all(parts, 'tensor', 0, 0)  63.4 us
    pallas_call x7, Pallas kernels, call(): pl.pallas_call(body, in_specs=[SMEM] * smem + [VMEM] * (len(args) - smem)...  46.4 us
    ppermute x39, waiting for transfers between devices, over(): return lax.ppermute(value, 'patch', pairs)  45.7 us
    all_to_all x2, waiting for transfers between devices, exchange(): return lax.all_to_all(parts, 'tensor', 0, 0)  30.4 us
    ppermute x39, starting transfers between devices, over(): return lax.ppermute(value, 'patch', pairs)  29.9 us
    all_to_all x3, waiting for transfers between devices, spread(): return lax.all_to_all(parts, 'tensor', 0, 0, axis_index_groups=COLUMNS)  29.4 us
    unnamed x79, local copies, waits for them, and re-layouts  26.7 us
    pallas_call x4, Pallas kernels, attend(): pl.pallas_call(functools.partial(attend_kernel, count, not state, last),...  22.5 us
  transfers between devices with their start and end apart: 47, of which 26 were waited for; matrix products, arithmetic and copies ran while one was open for 1% of the time, Pallas kernels for 14%

profile of v1, /device:TPU:0, one launch (start us, length us, event | category | flops | bytes accessed | tf_op | source)
XLA Modules:
  0.0 344.0 jit_solution(4704247575782637507)
XLA Ops:
  3.8 3.2 collective-permute-start.10
  13.3 5.4 %shard_map.185 = (f32[256,1024]{1,0:T(8,128)S(1)}, f32[256,64]{1,0:T(8,128)S(1)}, f32[256,128]{1,0:T(8,128)S(1)}, f32[256,192]{1,0:T(8,128)S(1)}) custom-call(s32[2]{0:T(128)S(1)} %pad_add_fusion.ids, f32[256,768]{1,0:T(8,128)S(1)} %copy-done.14, s32[2,768]{1,0:T(2,128)S(1)} %copy-done.29, f32[2,384,1024]{2,1,0:T(8,128)S(1)} %copy-done.10, ...), custom_call_target="tpu_custom_call" | custom-call | flops 3221225472 | bytes 7092232 | tf_op jit(solution)/shard_map/pallas_call | solution.py:134
  22.7 5.3 %all-to-all-start = ((f32[4,2,128,896]{3,2,1,0:T(8,128)}), f32[4,2,128,896]{3,2,1,0:T(8,128)}, u32[]{:S(2)}, u32[]{:S(2)}) async-start(f32[4,2,128,896]{3,2,1,0:T(8,128)} %broadcast_in_dim.33), calls=%async_computation | async-start | bytes 7340032 | tf_op jit(solution)/shard_map/all_to_all | solution.py:68
  31.9 5.5 %collective-permute-done.5.refs_1_ = f32[512,128]{1,0:T(8,128)S(1)} collective-permute-done((f32[512,128]{1,0:T(8,128)S(1)}, f32[512,128]{1,0:T(8,128)S(1)}, u32[]{:S(2)}, u32[]{:S(2)}) %collective-permute-start.5) | collective-permute-done | bytes 262176 | tf_op jit(solution)/shard_map/ppermute | solution.py:40
  44.8 4.2 %attend.4 = (f32[512,64]{1,0:T(8,128)S(1)}, f32[512,1]{1,0:T(8,128)S(1)}, f32[512,1]{1,0:T(8,128)S(1)}) custom-call(f32[512,64]{1,0:T(8,128)S(1)} %pad_maximum_fusion.3.q_ref, f32[512,128]{1,0:T(8,128)S(1)} %pad_maximum_fusion.4.refs_0_, f32[512,128]{1,0:T(8,128)S(1)} %collective-permute-done.5.refs_1_, f32[512,128]{1,0:T(8,128)S(1)} %collective-permute-done.3.refs_2_, ...), custom_call_target="tpu_custom_call" | custom-call | flops 4294967296 | bytes 1048576 | tf_op jit(solution)/shard_map/attend/pallas_call | solution.py:276
  50.1 3.2 collective-permute-done.8.refs_3_
  53.3 7.0 %attend.5 = f32[512,64]{1,0:T(8,128)S(1)} custom-call(f32[512,64]{1,0:T(8,128)S(1)} %pad_maximum_fusion.3.q_ref, f32[512,128]{1,0:T(8,128)S(1)} %collective-permute-done.2.refs_0_, f32[512,128]{1,0:T(8,128)S(1)} %collective-permute-done.4.refs_1_, f32[512,128]{1,0:T(8,128)S(1)} %constant_dynamic-update-slice_fusion.refs_2_, ...), custom_call_target="tpu_custom_call" | custom-call | flops 4294967296 | bytes 1048576 | tf_op jit(solution)/shard_map/attend/pallas_call | solution.py:276
  62.0 10.1 %all-to-all-done = f32[4,2,128,896]{3,2,1,0:T(8,128)} async-done(((f32[4,2,128,896]{3,2,1,0:T(8,128)}), f32[4,2,128,896]{3,2,1,0:T(8,128)}, u32[]{:S(2)}, u32[]{:S(2)}) %all-to-all-start) | async-done | bytes 3670048 | tf_op jit(solution)/shard_map/all_to_all | solution.py:68
  72.2 20.6 %all_to_all.40.m_ref = f32[8,256,128]{2,1,0:T(8,128)S(1)} all-to-all(f32[8,256,128]{2,1,0:T(8,128)S(1)} %broadcast_in_dim.34), channel_id=1, replica_groups=mesh['patch'=16,'tensor'=8] {'tensor'}, dimensions={0} | all-to-all | bytes 2097152 | tf_op jit(solution)/shard_map/all_to_all | solution.py:58
  95.0 8.8 %shard_map.186 = (f32[256,768]{1,0:T(8,128)S(1)}, f32[256,1]{1,0:T(8,128)S(1)}) custom-call(s32[2]{0:T(128)S(1)} %pad_add_fusion.ids, f32[8,256,128]{2,1,0:T(8,128)S(1)} %all_to_all.40.m_ref, f32[8,128,896]{2,1,0:T(8,128)} %bitcast.22.own_ref, f32[8,128,896]{2,1,0:T(8,128)S(1)} %bitcast.44, f32[256,1024]{1,0:T(8,128)S(1)} %copy-done.32, ...), custom_call_target="tpu_custom_call" | custom-call | flops 6442450944 | bytes 10237960 | tf_op jit(solution)/shard_map/pallas_call | solution.py:134
  103.9 5.4 %shard_map.187 = (f32[256,1024]{1,0:T(8,128)S(1)}, f32[256,64]{1,0:T(8,128)S(1)}, f32[256,128]{1,0:T(8,128)S(1)}, f32[256,192]{1,0:T(8,128)S(1)}) custom-call(s32[2]{0:T(128)S(1)} %pad_add_fusion.ids, f32[256,768]{1,0:T(8,128)S(1)} %get-tuple-element.48.field_ref, s32[2,768]{1,0:T(2,128)S(1)} %copy-done.30, f32[2,384,1024]{2,1,0:T(8,128)S(1)} %copy-done.11, ...), custom_call_target="tpu_custom_call" | custom-call | flops 3221225472 | bytes 7092232 | tf_op jit(solution)/shard_map/pallas_call | solution.py:134
  113.4 4.7 %all-to-all-start.2 = ((f32[4,2,128,896]{3,2,1,0:T(8,128)}), f32[4,2,128,896]{3,2,1,0:T(8,128)}, u32[]{:S(2)}, u32[]{:S(2)}) async-start(f32[4,2,128,896]{3,2,1,0:T(8,128)} %broadcast_in_dim.35), calls=%async_computation.2 | async-start | bytes 7340032 | tf_op jit(solution)/shard_map/all_to_all | solution.py:68
  122.1 5.7 %collective-permute-done.17.refs_1_ = f32[512,128]{1,0:T(8,128)S(1)} collective-permute-done((f32[512,128]{1,0:T(8,128)S(1)}, f32[512,128]{1,0:T(8,128)S(1)}, u32[]{:S(2)}, u32[]{:S(2)}) %collective-permute-start.17) | collective-permute-done | bytes 262176 | tf_op jit(solution)/shard_map/ppermute | solution.py:40
  135.1 4.2 %attend.6 = (f32[512,64]{1,0:T(8,128)S(1)}, f32[512,1]{1,0:T(8,128)S(1)}, f32[512,1]{1,0:T(8,128)S(1)}) custom-call(f32[512,64]{1,0:T(8,128)S(1)} %pad_maximum_fusion.5.q_ref, f32[512,128]{1,0:T(8,128)S(1)} %pad_maximum_fusion.6.refs_0_, f32[512,128]{1,0:T(8,128)S(1)} %collective-permute-done.17.refs_1_, f32[512,128]{1,0:T(8,128)S(1)} %collective-permute-done.15.refs_2_, ...), custom_call_target="tpu_custom_call" | custom-call | flops 4294967296 | bytes 1048576 | tf_op jit(solution)/shard_map/attend/pallas_call | solution.py:276
  140.5 3.5 %collective-permute-done.20.refs_3_ = f32[512,128]{1,0:T(8,128)S(1)} collective-permute-done((f32[512,128]{1,0:T(8,128)S(1)}, f32[512,128]{1,0:T(8,128)S(1)}, u32[]{:S(2)}, u32[]{:S(2)}) %collective-permute-start.20) | collective-permute-done | bytes 262176 | tf_op jit(solution)/shard_map/ppermute | solution.py:40
  144.1 7.0 %attend.7 = f32[512,64]{1,0:T(8,128)S(1)} custom-call(f32[512,64]{1,0:T(8,128)S(1)} %pad_maximum_fusion.5.q_ref, f32[512,128]{1,0:T(8,128)S(1)} %collective-permute-done.14.refs_0_, f32[512,128]{1,0:T(8,128)S(1)} %collective-permute-done.16.refs_1_, f32[512,128]{1,0:T(8,128)S(1)} %constant_dynamic-update-slice_fusion.2.refs_2_, ...), custom_call_target="tpu_custom_call" | custom-call | flops 4294967296 | bytes 1048576 | tf_op jit(solution)/shard_map/attend/pallas_call | solution.py:276
  152.7 9.3 %all-to-all-done.2 = f32[4,2,128,896]{3,2,1,0:T(8,128)} async-done(((f32[4,2,128,896]{3,2,1,0:T(8,128)}), f32[4,2,128,896]{3,2,1,0:T(8,128)}, u32[]{:S(2)}, u32[]{:S(2)}) %all-to-all-start.2) | async-done | bytes 3670048 | tf_op jit(solution)/shard_map/all_to_all | solution.py:68
  162.0 22.2 %all_to_all.41.m_ref = f32[8,256,128]{2,1,0:T(8,128)S(1)} all-to-all(f32[8,256,128]{2,1,0:T(8,128)S(1)} %broadcast_in_dim.36), channel_id=1, replica_groups=mesh['patch'=16,'tensor'=8] {'tensor'}, dimensions={0} | all-to-all | bytes 2097152 | tf_op jit(solution)/shard_map/all_to_all | solution.py:58
  185.4 8.8 %shard_map.188 = (bf16[256,768]{1,0:T(8,128)(2,1)S(1)}, f32[256,1]{1,0:T(8,128)S(1)}) custom-call(s32[2]{0:T(128)S(1)} %pad_add_fusion.ids, f32[8,256,128]{2,1,0:T(8,128)S(1)} %all_to_all.41.m_ref, f32[8,128,896]{2,1,0:T(8,128)} %bitcast.26.own_ref, f32[8,128,896]{2,1,0:T(8,128)S(1)} %bitcast.45, f32[256,1024]{1,0:T(8,128)S(1)} %copy-done.34, ...), custom_call_target="tpu_custom_call" | custom-call | flops 6442450944 | bytes 10237960 | tf_op jit(solution)/shard_map/pallas_call | solution.py:134
  195.5 3.6 %all-to-all-start.4 = ((bf16[8,256,256]{2,1,0:T(8,128)(2,1)}), bf16[8,256,256]{2,1,0:T(8,128)(2,1)S(1)}, u32[]{:S(2)}, u32[]{:S(2)}) async-start(bf16[8,256,256]{2,1,0:T(8,128)(2,1)} %broadcast_in_dim.37), calls=%async_computation.4 | async-start | bytes 2097152 | tf_op jit(solution)/shard_map/all_to_all | solution.py:58
  199.9 3.6 %collective-permute-start.40 = (bf16[256,1024]{1,0:T(8,128)(2,1)}, bf16[256,1024]{1,0:T(8,128)(2,1)}, u32[]{:S(2)}, u32[]{:S(2)}) collective-permute-start(bf16[256,1024]{1,0:T(8,128)(2,1)} %constant_dynamic-slice_fusion), channel_id=1, source_target_pairs={{0,1},{1,0},{2,3},{3,2},{4,5},{5,4},{6,7},{7,6},{8,9},{9,8},{10,11... | collective-permute-start | bytes 1572872 | tf_op jit(solution)/shard_map/ppermute | solution.py:482
  203.6 14.0 %all-to-all-done.4.emb_ref = bf16[8,256,256]{2,1,0:T(8,128)(2,1)S(1)} async-done(((bf16[8,256,256]{2,1,0:T(8,128)(2,1)}), bf16[8,256,256]{2,1,0:T(8,128)(2,1)S(1)}, u32[]{:S(2)}, u32[]{:S(2)}) %all-to-all-start.4) | async-done | bytes 1048608 | tf_op jit(solution)/shard_map/all_to_all | solution.py:58
  221.0 4.2 %collective-permute-done.40 = bf16[256,1024]{1,0:T(8,128)(2,1)} collective-permute-done((bf16[256,1024]{1,0:T(8,128)(2,1)}, bf16[256,1024]{1,0:T(8,128)(2,1)}, u32[]{:S(2)}, u32[]{:S(2)}) %collective-permute-start.40) | collective-permute-done | bytes 524320 | tf_op jit(solution)/shard_map/ppermute | solution.py:482
  229.1 5.0 %all-to-all-start.5 = ((bf16[4,2,256,1024]{3,2,1,0:T(8,128)(2,1)}), bf16[4,2,256,1024]{3,2,1,0:T(8,128)(2,1)}, u32[]{:S(2)}, u32[]{:S(2)}) async-start(bf16[4,2,256,1024]{3,2,1,0:T(8,128)(2,1)} %broadcast_in_dim.41), calls=%async_computation.5 | async-start | bytes 8388608 | tf_op jit(solution)/shard_map/all_to_all | solution.py:68
  238.0 4.1 %collective-permute-done.24.refs_1_ = bf16[256,512]{1,0:T(8,128)(2,1)S(1)} collective-permute-done((bf16[256,512]{1,0:T(8,128)(2,1)S(1)}, bf16[256,512]{1,0:T(8,128)(2,1)S(1)}, u32[]{:S(2)}, u32[]{:S(2)}) %collective-permute-start.24) | collective-permute-done | bytes 262176 | tf_op jit(solution)/shard_map/ppermute | solution.py:40
  251.5 7.7 %collective-permute-done.27.refs_4_ = bf16[256,512]{1,0:T(8,128)(2,1)} collective-permute-done((bf16[256,512]{1,0:T(8,128)(2,1)}, bf16[256,512]{1,0:T(8,128)(2,1)}, u32[]{:S(2)}, u32[]{:S(2)}) %collective-permute-start.27) | collective-permute-done | bytes 262176 | tf_op jit(solution)/shard_map/ppermute | solution.py:40
  267.3 4.5 %shard_map.190 = bf16[256,256]{1,0:T(8,128)(2,1)S(1)} custom-call(s32[18]{0:T(128)S(1)} %stack.111.ids, bf16[256,256]{1,0:T(8,128)(2,1)S(1)} %get-tuple-element.62.q_ref, s32[256,1]{1,0:T(8,128)S(1)} %copy.20.order_ref, s32[1,256]{1,0:T(1,128)S(1)} %bitcast.42, bf16[256,512]{1,0:T(8,128)(2,1)S(1)} %copy-done.18, ...), custom_call_target="tpu_custom_call" | custom-call | flops 2147483648 | bytes 4327496 | tf_op jit(solution)/shard_map/pallas_call | solution.py:134
  271.9 10.0 %all-to-all-done.5 = bf16[4,2,256,1024]{3,2,1,0:T(8,128)(2,1)} async-done(((bf16[4,2,256,1024]{3,2,1,0:T(8,128)(2,1)}), bf16[4,2,256,1024]{3,2,1,0:T(8,128)(2,1)}, u32[]{:S(2)}, u32[]{:S(2)}) %all-to-all-start.5) | async-done | bytes 4194336 | tf_op jit(solution)/shard_map/all_to_all | solution.py:68
  281.9 20.6 %all_to_all.42.att_ref = bf16[8,256,256]{2,1,0:T(8,128)(2,1)S(1)} all-to-all(bf16[8,256,256]{2,1,0:T(8,128)(2,1)S(1)} %broadcast_in_dim.42), channel_id=1, replica_groups=mesh['patch'=16,'tensor'=8] {'tensor'}, dimensions={0} | all-to-all | bytes 2097152 | tf_op jit(solution)/shard_map/all_to_all | solution.py:58
  309.8 12.3 %shard_map.191 = (bf16[8,256,256]{2,1,0:T(8,128)(2,1)}, f32[256,256]{1,0:T(8,128)S(1)}) custom-call(s32[2]{0:T(128)S(1)} %pad_add_fusion.ids, bf16[8,256,256]{2,1,0:T(8,128)(2,1)S(1)} %all_to_all.42.att_ref, bf16[8,256,256]{2,1,0:T(8,128)(2,1)S(1)} %all-to-all-done.4.emb_ref, bf16[8,256,1024]{2,1,0:T(8,128)(2,1)} %bitcast.33.own_ref, ...), custom_call_target="tpu_custom_call" | custom-call | flops 6442450944 | bytes 23076872 | tf_op jit(solution)/shard_map/pallas_call | solution.py:134
  322.1 3.6 %all-to-all-start.7 = ((bf16[8,256,256]{2,1,0:T(8,128)(2,1)}), bf16[8,256,256]{2,1,0:T(8,128)(2,1)S(1)}, u32[]{:S(2)}, u32[]{:S(2)}) async-start(bf16[8,256,256]{2,1,0:T(8,128)(2,1)} %get-tuple-element.68), calls=%async_computation.7 | async-start | bytes 2097152 | tf_op jit(solution)/shard_map/all_to_all | solution.py:58
  326.4 16.4 %all-to-all-done.7 = bf16[8,256,256]{2,1,0:T(8,128)(2,1)S(1)} async-done(((bf16[8,256,256]{2,1,0:T(8,128)(2,1)}), bf16[8,256,256]{2,1,0:T(8,128)(2,1)S(1)}, u32[]{:S(2)}, u32[]{:S(2)}) %all-to-all-start.7) | async-done | bytes 1048608 | tf_op jit(solution)/shard_map/all_to_all | solution.py:58
  (197 shorter events, 88.4 us)
Async XLA Ops:
  3.8 16.7 %collective-permute-start.10 = (f32[128,896]{1,0:T(8,128)S(1)}, f32[128,896]{1,0:T(8,128)S(1)}, u32[]{:S(2)}, u32[]{:S(2)}) collective-permute-start(f32[128,896]{1,0:T(8,128)S(1)} %get-tuple-element.44), channel_id=1, source_target_pairs={{0,1},{1,0},{2,3},{3,2},{4,5},{5,4},{6,7},{7,6},{8,9},{9,8},{10,11... | collective-permute-start | bytes 1376264 | tf_op jit(solution)/shard_map/ppermute | solution.py:456
  22.7 49.4 %all-to-all-start = ((f32[4,2,128,896]{3,2,1,0:T(8,128)}), f32[4,2,128,896]{3,2,1,0:T(8,128)}, u32[]{:S(2)}, u32[]{:S(2)}) async-start(f32[4,2,128,896]{3,2,1,0:T(8,128)} %broadcast_in_dim.33), calls=%async_computation | async-start | bytes 7340032 | tf_op jit(solution)/shard_map/all_to_all | solution.py:68
  28.1 9.3 %collective-permute-start.5 = (f32[512,128]{1,0:T(8,128)S(1)}, f32[512,128]{1,0:T(8,128)S(1)}, u32[]{:S(2)}, u32[]{:S(2)}) collective-permute-start(f32[512,128]{1,0:T(8,128)S(1)} %pad_maximum_fusion.4.refs_0_), channel_id=1, source_target_pairs={{0,32},{8,40},{16,48},{24,56},{32,64},{40,72},{48,80},{56,88},{64,... | collective-permute-start | bytes 786440 | tf_op jit(solution)/shard_map/ppermute | solution.py:40
  29.6 8.2 %collective-permute-start.3 = (f32[512,128]{1,0:T(8,128)S(1)}, f32[512,128]{1,0:T(8,128)S(1)}, u32[]{:S(2)}, u32[]{:S(2)}) collective-permute-start(f32[512,128]{1,0:T(8,128)S(1)} %pad_maximum_fusion.4.refs_0_), channel_id=1, source_target_pairs={{0,96},{8,104},{16,112},{24,120},{32,0},{40,8},{48,16},{56,24},{64... | collective-permute-start | bytes 786440 | tf_op jit(solution)/shard_map/ppermute | solution.py:40
  31.3 10.2 %collective-permute-start.1 = (f32[512,128]{1,0:T(8,128)S(1)}, f32[512,128]{1,0:T(8,128)S(1)}, u32[]{:S(2)}, u32[]{:S(2)}) collective-permute-start(f32[512,128]{1,0:T(8,128)S(1)} %pad_maximum_fusion.4.refs_0_), channel_id=1, source_target_pairs={{0,16},{8,24},{16,0},{24,8},{32,48},{40,56},{48,32},{56,40},{64,80... | collective-permute-start | bytes 786440 | tf_op jit(solution)/shard_map/ppermute | solution.py:40
  40.8 9.3 %collective-permute-start.4 = (f32[512,128]{1,0:T(8,128)S(1)}, f32[512,128]{1,0:T(8,128)S(1)}, u32[]{:S(2)}, u32[]{:S(2)}) collective-permute-start(f32[512,128]{1,0:T(8,128)S(1)} %collective-permute-done.3.refs_2_), channel_id=1, source_target_pairs={{0,16},{8,24},{16,0},{24,8},{32,48},{40,56},{48,32},{56,40},{64,80... | collective-permute-start | bytes 786440 | tf_op jit(solution)/shard_map/ppermute | solution.py:40
  41.5 7.7 %collective-permute-start.2 = (f32[512,128]{1,0:T(8,128)S(1)}, f32[512,128]{1,0:T(8,128)S(1)}, u32[]{:S(2)}, u32[]{:S(2)}) collective-permute-start(f32[512,128]{1,0:T(8,128)S(1)} %collective-permute-done.1.refs_3_), channel_id=1, source_target_pairs={{0,32},{8,40},{16,48},{24,56},{32,64},{40,72},{48,80},{56,88},{64,... | collective-permute-start | bytes 786440 | tf_op jit(solution)/shard_map/ppermute | solution.py:40
  43.7 9.6 %collective-permute-start.8 = (f32[512,128]{1,0:T(8,128)S(1)}, f32[512,128]{1,0:T(8,128)S(1)}, u32[]{:S(2)}, u32[]{:S(2)}) collective-permute-start(f32[512,128]{1,0:T(8,128)S(1)} %constant_dynamic-update-slice_fusion.refs_2_), channel_id=1, source_target_pairs={{0,16},{8,24},{16,0},{24,8},{32,48},{40,56},{48,32},{56,40},{64,80... | collective-permute-start | bytes 786440 | tf_op jit(solution)/shard_map/ppermute | solution.py:40
  72.1 21.7 %collective-permute-start.11 = (f32[4,2,128,896]{3,2,1,0:T(8,128)}, f32[4,2,128,896]{3,2,1,0:T(8,128)S(1)}, u32[]{:S(2)}, u32[]{:S(2)}) collective-permute-start(f32[4,2,128,896]{3,2,1,0:T(8,128)} %all-to-all-done), channel_id=1, source_target_pairs={{0,8},{8,0},{16,24},{24,16},{32,40},{40,32},{48,56},{56,48},{64,72... | collective-permute-start | bytes 11010056 | tf_op jit(solution)/shard_map/ppermute | solution.py:40
  92.8 18.4 %collective-permute-start.22 = (f32[128,896]{1,0:T(8,128)S(1)}, f32[128,896]{1,0:T(8,128)S(1)}, u32[]{:S(2)}, u32[]{:S(2)}) collective-permute-start(f32[128,896]{1,0:T(8,128)S(1)} %get-tuple-element.57), channel_id=1, source_target_pairs={{0,1},{1,0},{2,3},{3,2},{4,5},{5,4},{6,7},{7,6},{8,9},{9,8},{10,11... | collective-permute-start | bytes 1376264 | tf_op jit(solution)/shard_map/ppermute | solution.py:479
  113.4 48.6 %all-to-all-start.2 = ((f32[4,2,128,896]{3,2,1,0:T(8,128)}), f32[4,2,128,896]{3,2,1,0:T(8,128)}, u32[]{:S(2)}, u32[]{:S(2)}) async-start(f32[4,2,128,896]{3,2,1,0:T(8,128)} %broadcast_in_dim.35), calls=%async_computation.2 | async-start | bytes 7340032 | tf_op jit(solution)/shard_map/all_to_all | solution.py:68
  118.1 9.7 %collective-permute-start.17 = (f32[512,128]{1,0:T(8,128)S(1)}, f32[512,128]{1,0:T(8,128)S(1)}, u32[]{:S(2)}, u32[]{:S(2)}) collective-permute-start(f32[512,128]{1,0:T(8,128)S(1)} %pad_maximum_fusion.6.refs_0_), channel_id=1, source_target_pairs={{0,32},{8,40},{16,48},{24,56},{32,64},{40,72},{48,80},{56,88},{64,... | collective-permute-start | bytes 786440 | tf_op jit(solution)/shard_map/ppermute | solution.py:40
  119.8 8.4 %collective-permute-start.15 = (f32[512,128]{1,0:T(8,128)S(1)}, f32[512,128]{1,0:T(8,128)S(1)}, u32[]{:S(2)}, u32[]{:S(2)}) collective-permute-start(f32[512,128]{1,0:T(8,128)S(1)} %pad_maximum_fusion.6.refs_0_), channel_id=1, source_target_pairs={{0,96},{8,104},{16,112},{24,120},{32,0},{40,8},{48,16},{56,24},{64... | collective-permute-start | bytes 786440 | tf_op jit(solution)/shard_map/ppermute | solution.py:40
  121.4 10.6 %collective-permute-start.13 = (f32[512,128]{1,0:T(8,128)S(1)}, f32[512,128]{1,0:T(8,128)S(1)}, u32[]{:S(2)}, u32[]{:S(2)}) collective-permute-start(f32[512,128]{1,0:T(8,128)S(1)} %pad_maximum_fusion.6.refs_0_), channel_id=1, source_target_pairs={{0,16},{8,24},{16,0},{24,8},{32,48},{40,56},{48,32},{56,40},{64,80... | collective-permute-start | bytes 786440 | tf_op jit(solution)/shard_map/ppermute | solution.py:40
  131.3 9.3 %collective-permute-start.16 = (f32[512,128]{1,0:T(8,128)S(1)}, f32[512,128]{1,0:T(8,128)S(1)}, u32[]{:S(2)}, u32[]{:S(2)}) collective-permute-start(f32[512,128]{1,0:T(8,128)S(1)} %collective-permute-done.15.refs_2_), channel_id=1, source_target_pairs={{0,16},{8,24},{16,0},{24,8},{32,48},{40,56},{48,32},{56,40},{64,80... | collective-permute-start | bytes 786440 | tf_op jit(solution)/shard_map/ppermute | solution.py:40
  132.0 8.0 %collective-permute-start.14 = (f32[512,128]{1,0:T(8,128)S(1)}, f32[512,128]{1,0:T(8,128)S(1)}, u32[]{:S(2)}, u32[]{:S(2)}) collective-permute-start(f32[512,128]{1,0:T(8,128)S(1)} %collective-permute-done.13.refs_3_), channel_id=1, source_target_pairs={{0,32},{8,40},{16,48},{24,56},{32,64},{40,72},{48,80},{56,88},{64,... | collective-permute-start | bytes 786440 | tf_op jit(solution)/shard_map/ppermute | solution.py:40
  134.1 9.9 %collective-permute-start.20 = (f32[512,128]{1,0:T(8,128)S(1)}, f32[512,128]{1,0:T(8,128)S(1)}, u32[]{:S(2)}, u32[]{:S(2)}) collective-permute-start(f32[512,128]{1,0:T(8,128)S(1)} %constant_dynamic-update-slice_fusion.2.refs_2_), channel_id=1, source_target_pairs={{0,16},{8,24},{16,0},{24,8},{32,48},{40,56},{48,32},{56,40},{64,80... | collective-permute-start | bytes 786440 | tf_op jit(solution)/shard_map/ppermute | solution.py:40
  162.0 22.3 %collective-permute-start.23 = (f32[4,2,128,896]{3,2,1,0:T(8,128)}, f32[4,2,128,896]{3,2,1,0:T(8,128)S(1)}, u32[]{:S(2)}, u32[]{:S(2)}) collective-permute-start(f32[4,2,128,896]{3,2,1,0:T(8,128)} %all-to-all-done.2), channel_id=1, source_target_pairs={{0,8},{8,0},{16,24},{24,16},{32,40},{40,32},{48,56},{56,48},{64,72... | collective-permute-start | bytes 11010056 | tf_op jit(solution)/shard_map/ppermute | solution.py:40
  195.5 22.1 %all-to-all-start.4 = ((bf16[8,256,256]{2,1,0:T(8,128)(2,1)}), bf16[8,256,256]{2,1,0:T(8,128)(2,1)S(1)}, u32[]{:S(2)}, u32[]{:S(2)}) async-start(bf16[8,256,256]{2,1,0:T(8,128)(2,1)} %broadcast_in_dim.37), calls=%async_computation.4 | async-start | bytes 2097152 | tf_op jit(solution)/shard_map/all_to_all | solution.py:58
  199.9 25.3 %collective-permute-start.40 = (bf16[256,1024]{1,0:T(8,128)(2,1)}, bf16[256,1024]{1,0:T(8,128)(2,1)}, u32[]{:S(2)}, u32[]{:S(2)}) collective-permute-start(bf16[256,1024]{1,0:T(8,128)(2,1)} %constant_dynamic-slice_fusion), channel_id=1, source_target_pairs={{0,1},{1,0},{2,3},{3,2},{4,5},{5,4},{6,7},{7,6},{8,9},{9,8},{10,11... | collective-permute-start | bytes 1572872 | tf_op jit(solution)/shard_map/ppermute | solution.py:482
  229.1 52.8 %all-to-all-start.5 = ((bf16[4,2,256,1024]{3,2,1,0:T(8,128)(2,1)}), bf16[4,2,256,1024]{3,2,1,0:T(8,128)(2,1)}, u32[]{:S(2)}, u32[]{:S(2)}) async-start(bf16[4,2,256,1024]{3,2,1,0:T(8,128)(2,1)} %broadcast_in_dim.41), calls=%async_computation.5 | async-start | bytes 8388608 | tf_op jit(solution)/shard_map/all_to_all | solution.py:68
  234.0 8.1 %collective-permute-start.24 = (bf16[256,512]{1,0:T(8,128)(2,1)S(1)}, bf16[256,512]{1,0:T(8,128)(2,1)S(1)}, u32[]{:S(2)}, u32[]{:S(2)}) collective-permute-start(bf16[256,512]{1,0:T(8,128)(2,1)S(1)} %copy-done.17), channel_id=1, source_target_pairs={{0,32},{8,40},{16,48},{24,56},{32,64},{40,72},{48,80},{56,88},{64,... | collective-permute-start | bytes 786440 | tf_op jit(solution)/shard_map/ppermute | solution.py:40
  235.7 6.8 %collective-permute-start.25 = (bf16[256,512]{1,0:T(8,128)(2,1)S(1)}, bf16[256,512]{1,0:T(8,128)(2,1)S(1)}, u32[]{:S(2)}, u32[]{:S(2)}) collective-permute-start(bf16[256,512]{1,0:T(8,128)(2,1)S(1)} %copy-done.17), channel_id=1, source_target_pairs={{0,96},{8,104},{16,112},{24,120},{32,0},{40,8},{48,16},{56,24},{64... | collective-permute-start | bytes 786440 | tf_op jit(solution)/shard_map/ppermute | solution.py:40
  237.4 11.0 %collective-permute-start.26 = (bf16[256,512]{1,0:T(8,128)(2,1)S(1)}, bf16[256,512]{1,0:T(8,128)(2,1)}, u32[]{:S(2)}, u32[]{:S(2)}) collective-permute-start(bf16[256,512]{1,0:T(8,128)(2,1)S(1)} %copy-done.17), channel_id=1, source_target_pairs={{0,16},{8,24},{16,0},{24,8},{32,48},{40,56},{48,32},{56,40},{64,80... | collective-permute-start | bytes 786440 | tf_op jit(solution)/shard_map/ppermute | solution.py:40
  242.5 7.6 %collective-permute-start.32 = (bf16[256,512]{1,0:T(8,128)(2,1)S(1)}, bf16[256,512]{1,0:T(8,128)(2,1)S(1)}, u32[]{:S(2)}, u32[]{:S(2)}) collective-permute-start(bf16[256,512]{1,0:T(8,128)(2,1)S(1)} %copy-done.17), channel_id=1, source_target_pairs={{0,8},{8,0},{16,24},{24,16},{32,40},{40,32},{48,56},{56,48},{64,72... | collective-permute-start | bytes 786440 | tf_op jit(solution)/shard_map/ppermute | solution.py:40
  245.5 13.7 %collective-permute-start.28 = (bf16[256,512]{1,0:T(8,128)(2,1)S(1)}, bf16[256,512]{1,0:T(8,128)(2,1)}, u32[]{:S(2)}, u32[]{:S(2)}) collective-permute-start(bf16[256,512]{1,0:T(8,128)(2,1)S(1)} %collective-permute-done.25.refs_2_), channel_id=1, source_target_pairs={{0,16},{8,24},{16,0},{24,8},{32,48},{40,56},{48,32},{56,40},{64,80... | collective-permute-start | bytes 786440 | tf_op jit(solution)/shard_map/ppermute | solution.py:40
  248.4 11.3 %collective-permute-start.33 = (bf16[256,512]{1,0:T(8,128)(2,1)S(1)}, bf16[256,512]{1,0:T(8,128)(2,1)S(1)}, u32[]{:S(2)}, u32[]{:S(2)}) collective-permute-start(bf16[256,512]{1,0:T(8,128)(2,1)S(1)} %collective-permute-done.24.refs_1_), channel_id=1, source_target_pairs={{0,8},{8,0},{16,24},{24,16},{32,40},{40,32},{48,56},{56,48},{64,72... | collective-permute-start | bytes 786440 | tf_op jit(solution)/shard_map/ppermute | solution.py:40
  248.4 12.0 %collective-permute-start.34 = (bf16[256,512]{1,0:T(8,128)(2,1)S(1)}, bf16[256,512]{1,0:T(8,128)(2,1)S(1)}, u32[]{:S(2)}, u32[]{:S(2)}) collective-permute-start(bf16[256,512]{1,0:T(8,128)(2,1)S(1)} %collective-permute-done.25.refs_2_), channel_id=1, source_target_pairs={{0,8},{8,0},{16,24},{24,16},{32,40},{40,32},{48,56},{56,48},{64,72... | collective-permute-start | bytes 786440 | tf_op jit(solution)/shard_map/ppermute | solution.py:40
  249.0 10.2 %collective-permute-start.27 = (bf16[256,512]{1,0:T(8,128)(2,1)}, bf16[256,512]{1,0:T(8,128)(2,1)}, u32[]{:S(2)}, u32[]{:S(2)}) collective-permute-start(bf16[256,512]{1,0:T(8,128)(2,1)} %collective-permute-done.26.refs_3_), channel_id=1, source_target_pairs={{0,32},{8,40},{16,48},{24,56},{32,64},{40,72},{48,80},{56,88},{64,... | collective-permute-start | bytes 786440 | tf_op jit(solution)/shard_map/ppermute | solution.py:40
  250.8 10.8 %collective-permute-start.31 = (bf16[256,512]{1,0:T(8,128)(2,1)S(1)}, bf16[256,512]{1,0:T(8,128)(2,1)}, u32[]{:S(2)}, u32[]{:S(2)}) collective-permute-start(bf16[256,512]{1,0:T(8,128)(2,1)S(1)} %constant_dynamic-update-slice_fusion.4.refs_6_), channel_id=1, source_target_pairs={{0,16},{8,24},{16,0},{24,8},{32,48},{40,56},{48,32},{56,40},{64,80... | collective-permute-start | bytes 786440 | tf_op jit(solution)/shard_map/ppermute | solution.py:40
  281.9 20.7 %collective-permute-start.41 = (bf16[4,2,256,1024]{3,2,1,0:T(8,128)(2,1)}, bf16[4,2,256,1024]{3,2,1,0:T(8,128)(2,1)S(1)}, u32[]{:S(2)}, u32[]{:S(2)}) collective-permute-start(bf16[4,2,256,1024]{3,2,1,0:T(8,128)(2,1)} %all-to-all-done.5), channel_id=1, source_target_pairs={{0,8},{8,0},{16,24},{24,16},{32,40},{40,32},{48,56},{56,48},{64,72... | collective-permute-start | bytes 12582920 | tf_op jit(solution)/shard_map/ppermute | solution.py:40
  322.1 20.6 %all-to-all-start.7 = ((bf16[8,256,256]{2,1,0:T(8,128)(2,1)}), bf16[8,256,256]{2,1,0:T(8,128)(2,1)S(1)}, u32[]{:S(2)}, u32[]{:S(2)}) async-start(bf16[8,256,256]{2,1,0:T(8,128)(2,1)} %get-tuple-element.68), calls=%async_computation.7 | async-start | bytes 2097152 | tf_op jit(solution)/shard_map/all_to_all | solution.py:58
  (53 other events, 541.7 us)
